TPU v7x, 512 devices: a whole 4x4x16 slice. The times are simulated.
512 devices in a mesh: dom: 64 (over y, z_hi, x, core), feat: 8 (over z_lo).
Axes of the slice: x: 4, y: 4, z: 16 (z_hi: 2, z_lo: 8; z = z_hi * 8 + z_lo), core: 2. Of those that a mesh axis runs over, the one named last changes fastest.
Arguments:
- features: bfloat16 [32768, 1024], P('dom', 'feat'), may hold values from -16 to 16
- weights: bfloat16 [2048, 1024], P(None, 'feat'), may hold values from -4 to 4
- send_rows: int32 [64, 64, 128], P('dom'), may hold values from -1 to 511, as said below
- remote_src: int32 [64, 64], P('dom'), may hold values from 0 to 63, each once within a row
- local_adj: bfloat16 [32768, 512], P('dom')
- remote_adj: bfloat16 [32768, 16, 128], P('dom')
- degree: int32 [32768], P('dom'), may hold values from 48 to 143
- cotangent: bfloat16 [32768, 1024], P('dom', 'feat'), may hold values from -6 to 6
Outputs:
- output: bfloat16 [32768, 1024], P('dom', 'feat')
- grad_input: bfloat16 [32768, 1024], P('dom', 'feat')
- grad_weights: float32 [2048, 1024], P('dom', 'feat')
Inputs may be any that keep to these rules, and one draw needn't show every extreme that they name: `send_rows`: each entry is a row of partition p or -1; in each block the used places come first and name distinct rows; a quarter or more of each block is used, and some block is full. `remote_src`: each row names every partition once.
All inputs are finite; a program needn't handle non-finite values.
Results may differ from a plain program's by a relative error of at most 0.01.
Values may be sent and summed in bfloat16 or wider, within the bound.
A program may use at most 64 MiB of HBM per device.

v0:
```python
import math

import jax
import jax.numpy as jnp
from jax import lax
from jax.sharding import PartitionSpec as P


def per_device(features, weights, send_rows, remote_src, local_adj, remote_adj, degree, cotangent):
    np_rows, feat_width = features.shape
    feat_count = lax.axis_size("feat")
    dom_count = lax.axis_size("dom")
    full_width = feat_width * feat_count
    tile_rows = remote_adj.shape[2]
    block_count = np_rows // tile_rows
    remote_span = remote_adj.shape[1] * tile_rows
    rows_out = send_rows[0]
    live_mask = rows_out >= 0
    safe_rows = jnp.where(live_mask, rows_out, 0)
    outgoing = jnp.where(live_mask[:, :, None], features[safe_rows], jnp.zeros((), jnp.bfloat16))
    halo_rows = lax.all_to_all(outgoing, "dom", split_axis=0, concat_axis=0, tiled=True)
    slot_order = remote_src[0]
    ordered = jnp.take(halo_rows, slot_order, axis=0).reshape(block_count, remote_span, feat_width)
    remote_tiles = remote_adj.reshape(block_count, tile_rows, remote_span)
    remote_sums = jnp.einsum(
        "bik,bkf->bif", remote_tiles, ordered, preferred_element_type=jnp.float32
    ).reshape(np_rows, feat_width)
    local_sums = jnp.dot(local_adj, features, preferred_element_type=jnp.float32)
    degree_col = degree.astype(jnp.float32)[:, None]
    aggregate = ((local_sums + remote_sums) / degree_col).astype(jnp.bfloat16)
    stacked = jnp.stack([features, aggregate], axis=1)
    weight_pair = weights.reshape(2, full_width, feat_width)
    gathered = lax.all_gather(stacked, "feat", axis=2, tiled=True)
    preact = jnp.einsum("rkc,kcf->rf", gathered, weight_pair, preferred_element_type=jnp.float32)
    output = jax.nn.silu(preact).astype(jnp.bfloat16)
    sigmoid_z = jax.nn.sigmoid(preact)
    grad_pre = (
        cotangent.astype(jnp.float32) * sigmoid_z * (1.0 + preact * (1.0 - sigmoid_z))
    ).astype(jnp.bfloat16)
    scaled_grad = (grad_pre.astype(jnp.float32) / degree_col).astype(jnp.bfloat16)
    back_ordered = jnp.einsum(
        "bik,bif->bkf",
        remote_tiles,
        scaled_grad.reshape(block_count, tile_rows, feat_width),
        preferred_element_type=jnp.float32,
    )
    back_ordered = back_ordered.reshape(slot_order.shape[0], tile_rows, feat_width).astype(
        jnp.bfloat16
    )
    returning = jnp.zeros_like(back_ordered).at[slot_order].set(back_ordered)
    arriving = lax.all_to_all(returning, "dom", split_axis=0, concat_axis=0, tiled=True)
    target_rows = jnp.where(live_mask, rows_out, np_rows).reshape(-1)
    neigh_grad = lax.dot_general(
        local_adj, scaled_grad, (((0,), (0,)), ((), ())), preferred_element_type=jnp.float32
    )
    neigh_grad = neigh_grad.at[target_rows].add(
        arriving.reshape(-1, feat_width).astype(jnp.float32), mode="drop"
    )
    neigh_grad = neigh_grad.astype(jnp.bfloat16)
    back_pair = jnp.stack([grad_pre, neigh_grad], axis=1)
    partial_terms = jnp.einsum(
        "rkf,kcf->rc", back_pair, weight_pair, preferred_element_type=jnp.float32
    )
    grad_input = lax.psum_scatter(partial_terms, "feat", scatter_dimension=1, tiled=True).astype(
        jnp.bfloat16
    )
    weight_scale = 1.0 / math.sqrt(dom_count * np_rows)
    combined = gathered.reshape(np_rows, 2 * full_width)
    summed = lax.psum_scatter(
        lax.dot_general(
            combined, grad_pre, (((0,), (0,)), ((), ())), preferred_element_type=jnp.float32
        ),
        "dom",
        scatter_dimension=0,
        tiled=True,
    )
    grad_weights = summed * weight_scale
    return (output, grad_input, grad_weights)


def solution(mesh):
    in_specs = (
        P("dom", "feat"),
        P(None, "feat"),
        P("dom", None, None),
        P("dom", None),
        P("dom", None),
        P("dom", None, None),
        P("dom"),
        P("dom", "feat"),
    )
    out_specs = (P("dom", "feat"), P("dom", "feat"), P("dom", "feat"))
    return jax.shard_map(
        per_device, mesh=mesh, in_specs=in_specs, out_specs=out_specs, check_vma=False
    )
```

profile of v0, /device:TPU:6, one launch (start us, length us, event | category | flops | bytes accessed | tf_op | source)
XLA Modules:
  0.0 959.8 jit_solution(17300601197789234725)
XLA Ops:
  8.8 22.8 %gather_fusion = bf16[8192,128]{1,0:T(8,128)(2,1)S(1)} fusion(bf16[512,128]{1,0:T(8,128)(2,1)} %param.8, s32[8192]{0:T(1024)S(1)} %fusion.10), kind=kCustom, calls=%fused_computation | custom fusion | bytes 4227072 | tf_op jit(solution)/shard_map/gather | solution.py:20
  31.6 2.6 broadcast_select_fusion
  34.2 21.6 %all-to-all-start = ((bf16[64,128,128]{2,1,0:T(8,128)(2,1)}), bf16[64,128,128]{2,1,0:T(8,128)(2,1)}, u32[]{:S(2)}, u32[]{:S(2)}) async-start(bf16[64,128,128]{2,1,0:T(8,128)(2,1)} %broadcast_select_fusion), calls=%async_computation | async-start | bytes 4194304 | tf_op jit(solution)/shard_map/all_to_all | solution.py:21
  57.2 2.8 reshape.130
  60.1 45.4 %all-to-all-done = bf16[64,128,128]{2,1,0:T(8,128)(2,1)} async-done(((bf16[64,128,128]{2,1,0:T(8,128)(2,1)}), bf16[64,128,128]{2,1,0:T(8,128)(2,1)}, u32[]{:S(2)}, u32[]{:S(2)}) %all-to-all-start) | async-done | bytes 2097184 | tf_op jit(solution)/shard_map/all_to_all | solution.py:21
  105.4 3.7 gather_fusion.1
  109.1 4.4 bitcast_select_fusion
  115.7 118.2 %all-gather.2.cloned.1.call-done = bf16[512,2,1024]{2,0,1:T(8,128)(2,1)} async-done(((bf16[512,2,128]{2,0,1:T(8,128)(2,1)}), bf16[512,2,1024]{2,0,1:T(8,128)(2,1)}) %all-gather.2.cloned.1.call-update) | async-done | bytes 2097168 | tf_op jit(solution)/shard_map/all_gather | solution.py:33
  233.9 3.0 divide_convert_fusion
  236.8 2.1 fusion.2
  238.9 3.0 copy.14
  241.9 1.8 broadcast_in_dim.39
  243.8 8.7 scatter_fusion
  252.4 9.2 all-to-all-start.1
  261.7 3.9 copy.16
  265.6 3.3 fusion.13
  269.1 1.3 convolution_bitcast_fusion.1
  270.5 32.2 %all-to-all-done.1 = bf16[64,128,128]{2,1,0:T(8,128)(2,1)S(1)} async-done(((bf16[64,128,128]{2,1,0:T(8,128)(2,1)}), bf16[64,128,128]{2,1,0:T(8,128)(2,1)S(1)}, u32[]{:S(2)}, u32[]{:S(2)}) %all-to-all-start.1) | async-done | bytes 2097184 | tf_op jit(solution)/shard_map/all_to_all | solution.py:51
  302.7 44.3 %scatter_custom_fusion.1 = f32[512,128]{1,0:T(8,128)S(1)} fusion(f32[512,128]{1,0:T(8,128)S(1)} %copy.15, s32[8192]{0:T(1024)S(1)} %bitcast.73, bf16[8192,128]{1,0:T(8,128)(2,1)S(1)} %bitcast.65), kind=kCustom, calls=%fused_computation.4 | custom fusion | flops 2097152 | bytes 2359296 | tf_op jit(solution)/shard_map/scatter-add | solution.py:56
  347.1 1.8 convolution_bitcast_fusion
  348.9 494.5 %reduce-scatter.5.cloned.1.call-done = f32[32,128]{1,0:T(8,128)} async-done(((f32[2048,128]{1,0:T(8,128)}), f32[32,128]{1,0:T(8,128)}) %reduce-scatter.5.cloned.1.call-update) | async-done | bytes 16400 | tf_op jit(solution)/shard_map/reduce_scatter | solution.py:69
  843.3 1.3 broadcast_multiply_fusion
  844.7 106.9 %reduce-scatter.3.cloned.1.call-done = f32[512,128]{1,0:T(8,128)} async-done(((f32[512,1024]{1,0:T(8,128)}), f32[512,128]{1,0:T(8,128)}) %reduce-scatter.3.cloned.1.call-update) | async-done | bytes 262160 | tf_op jit(solution)/shard_map/reduce_scatter | solution.py:64
  951.6 1.6 convert_element_type.55
  (37 shorter events, 5.5 us)
Async XLA Ops:
  7.2 226.7 %copy-start = (bf16[2048,128]{1,0:T(8,128)(2,1)S(1)}, bf16[2048,128]{1,0:T(8,128)(2,1)}, u32[]{:S(2)}) copy-start(bf16[2048,128]{1,0:T(8,128)(2,1)} %param.9) | copy-start | bytes 1572868
  34.2 22.1 %copy-start.6 = (s32[1,64]{1,0:T(1,128)S(1)}, s32[1,64]{1,0:T(1,128)}, u32[]{:S(2)}) copy-start(s32[1,64]{1,0:T(1,128)} %param.11) | copy-start | bytes 772
  34.2 22.9 %copy-start.4 = (s32[512]{0:T(512)S(1)}, s32[512]{0:T(512)}, u32[]{:S(2)}) copy-start(s32[512]{0:T(512)} %param.14) | copy-start | bytes 6148
  34.2 71.2 %all-to-all-start = ((bf16[64,128,128]{2,1,0:T(8,128)(2,1)}), bf16[64,128,128]{2,1,0:T(8,128)(2,1)}, u32[]{:S(2)}, u32[]{:S(2)}) async-start(bf16[64,128,128]{2,1,0:T(8,128)(2,1)} %broadcast_select_fusion), calls=%async_computation | async-start | bytes 4194304 | tf_op jit(solution)/shard_map/all_to_all | solution.py:21
  55.8 178.1 %all-gather.2.cloned.1.call-start = ((), (), s32[]{:S(2)}) async-start(), calls=%async_computation.4 | async-start | bytes 2359296 | tf_op jit(solution)/shard_map/all_gather | solution.py:33
  113.5 0.9 copy-start.1
  113.5 1.1 copy-start.2
  114.3 119.6 %copy-start.5 = (bf16[512,128]{1,0:T(8,128)(2,1)S(1)}, bf16[512,128]{1,0:T(8,128)(2,1)}, u32[]{:S(2)}) copy-start(bf16[512,128]{1,0:T(8,128)(2,1)} %param.15) | copy-start | bytes 393220
  252.4 50.3 %all-to-all-start.1 = ((bf16[64,128,128]{2,1,0:T(8,128)(2,1)}), bf16[64,128,128]{2,1,0:T(8,128)(2,1)S(1)}, u32[]{:S(2)}, u32[]{:S(2)}) async-start(bf16[64,128,128]{2,1,0:T(8,128)(2,1)} %scatter_fusion), calls=%async_computation.1 | async-start | bytes 4194304 | tf_op jit(solution)/shard_map/all_to_all | solution.py:51
  261.7 581.7 %reduce-scatter.5.cloned.1.call-start = ((), (), s32[]{:S(2)}) async-start(), calls=%async_computation.6 | async-start | bytes 1064960 | tf_op jit(solution)/shard_map/reduce_scatter | solution.py:69
  265.6 3.3 copy-start.3
  268.9 682.7 %reduce-scatter.3.cloned.1.call-start = ((), (), s32[]{:S(2)}) async-start(), calls=%async_computation.5 | async-start | bytes 2359296 | tf_op jit(solution)/shard_map/reduce_scatter | solution.py:64
Sparse Core Ops, SparseCore 0:
  115.8 118.0 all-gather.1
  269.1 574.2 reduce-scatter.4
  846.2 105.3 reduce-scatter.2
where the time goes:
time: 961 us; the launch traced here: 960 us
  waiting for transfers between devices  797 us (83%)
  other arithmetic  57.3 us (6%)
  local copies, waits for them, and re-layouts  48 us (5%)
  starting transfers between devices  30.9 us (3%)
  between operations  13.9 us (1%)
  matrix products  12.4 us (1%)
    reduce_scatter x1, waiting for transfers between devices, per_device(): lax.psum_scatter(lax.dot_general(combined, grad_pre, (((0,), (0,)), ((),...  494 us
    all_gather x1, waiting for transfers between devices, per_device(): gathered = lax.all_gather(stacked, 'feat', axis=2, tiled=True)  118 us
    reduce_scatter x1, waiting for transfers between devices, per_device(): lax.psum_scatter(partial_terms, 'feat', scatter_dimension=1, tiled=True)  107 us
    all_to_all x1, waiting for transfers between devices, per_device(): lax.all_to_all(outgoing, 'dom', split_axis=0, concat_axis=0, tiled=True)  45.4 us
    scatter-add x1, other arithmetic, per_device(): neigh_grad.at[target_rows]  44.3 us
    all_to_all x1, waiting for transfers between devices, per_device(): lax.all_to_all(returning, 'dom', split_axis=0, concat_axis=0, tiled=True)  32.2 us
    gather x1, local copies, waits for them, and re-layouts, per_device(): features[safe_rows]  22.8 us
    all_to_all x1, starting transfers between devices, per_device(): lax.all_to_all(outgoing, 'dom', split_axis=0, concat_axis=0, tiled=True)  21.6 us
  transfers between devices with their start and end apart: 5, of which 5 were waited for; matrix products, arithmetic and copies ran while one was open for 6% of the time, Pallas kernels for 0%

commit v1 on v0

v1 whole, which is shorter than its diff:
```python
import math

import jax
import jax.numpy as jnp
from jax import lax
from jax.experimental import pallas as pl
from jax.experimental.pallas import tpu as pltpu
from jax.sharding import PartitionSpec as P

BF = jnp.bfloat16
F32 = jnp.float32
VMEM_BYTES = 48 * 1024 * 1024
NT = (((1,), (1,)), ((), ()))


def vmem():
    return pl.BlockSpec(memory_space=pltpu.VMEM)


def smem():
    return pl.BlockSpec(memory_space=pltpu.SMEM)


def params():
    return pltpu.CompilerParams(vmem_limit_bytes=VMEM_BYTES)


def one_hot(rows, count):
    spots = lax.broadcasted_iota(jnp.int32, (count, rows.shape[1]), 0)
    return jnp.where(spots == rows, 1.0, 0.0).astype(BF)


def pack_kernel(ft_ref, rows_ref, out_ref):
    count = ft_ref.shape[2]
    for z in range(2):
        ft = ft_ref[z]

        def body(j, carry):
            picked = jnp.dot(ft, one_hot(rows_ref[j, pl.ds(z, 1), :], count), preferred_element_type=F32)
            out_ref[j, z] = picked.astype(BF)
            return carry

        lax.fori_loop(0, out_ref.shape[0], body, 0, unroll=4)


def agg_kernel(src_ref, local_ref, feat_ref, tiles_ref, halo_ref, deg_ref, agg_ref, ordered):
    blk = halo_ref.shape[1]
    blocks = local_ref.shape[0] // blk
    span = tiles_ref.shape[1] // blk

    def body(b, carry):
        for t in range(span):
            ordered[:, t * blk:(t + 1) * blk] = halo_ref[src_ref[b * span + t]]
        rows = pl.ds(pl.multiple_of(b * blk, blk), blk)
        sums = lax.dot_general(tiles_ref[rows, :], ordered[...], NT, preferred_element_type=F32)
        sums += jnp.dot(local_ref[rows, :], feat_ref[...], preferred_element_type=F32)
        agg_ref[rows, :] = (sums / deg_ref[rows, :]).astype(BF)
        return carry

    lax.fori_loop(0, blocks, body, 0)


def back_kernel(src_ref, scaled_t_ref, tiles_ref, back_ref):
    blk = back_ref.shape[1]
    blocks = scaled_t_ref.shape[1] // blk
    span = tiles_ref.shape[1] // blk
    for b in range(blocks):
        left = scaled_t_ref[:, b * blk:(b + 1) * blk]
        terms = jnp.dot(
            left, tiles_ref[b * blk:(b + 1) * blk, :], preferred_element_type=F32
        ).astype(BF)
        for t in range(span):
            back_ref[src_ref[b * span + t]] = terms[:, t * blk:(t + 1) * blk]


def unpack_kernel(rows_ref, arrived_ref, scaled_t_ref, local_ref, half_ref, own_ref, other_ref, total):
    count = local_ref.shape[1]
    half = half_ref[0]
    total[...] = jnp.zeros_like(total)
    for z in range(2):

        def body(j, carry):
            left = jnp.concatenate([arrived_ref[2 * j, z], arrived_ref[2 * j + 1, z]], axis=1)
            right = jnp.concatenate(
                [
                    one_hot(rows_ref[2 * j, pl.ds(z, 1), :], count),
                    one_hot(rows_ref[2 * j + 1, pl.ds(z, 1), :], count),
                ],
                axis=1,
            )
            total[z] += lax.dot_general(left, right, NT, preferred_element_type=F32)
            return carry

        lax.fori_loop(0, arrived_ref.shape[0] // 2, body, 0, unroll=2)
    local = jnp.dot(scaled_t_ref[...], local_ref[...], preferred_element_type=F32)
    own_ref[...] = local + total[half]
    other_ref[...] = total[1 - half].astype(BF)


def per_device(features, weights, send_rows, remote_src, local_adj, remote_adj, degree, cotangent):
    np_rows, width = features.shape
    feats = lax.axis_size("feat")
    doms = lax.axis_size("dom")
    blk = remote_adj.shape[2]
    span = remote_adj.shape[1] * blk
    half_count = doms // 2
    pair = 8
    half = (lax.axis_index("dom") // pair) % 2
    swaps = [(d, d ^ pair) for d in range(doms)]
    groups = [[d for d in range(doms) if (d // pair) % 2 == h] for h in range(2)]

    feat_t = features.T
    other_t = lax.ppermute(feat_t, "dom", swaps)
    rows_own = send_rows[0]
    rows_other = lax.ppermute(rows_own, "dom", swaps)

    def by_half(own, other):
        return jnp.where(half == 0, jnp.stack([own, other]), jnp.stack([other, own]))

    rows2 = by_half(rows_own, rows_other).reshape(2, doms // 16, 2, pair, blk)
    rows2 = jnp.where(half == 0, rows2[:, :, 0], rows2[:, :, 1]).reshape(2, half_count, blk)
    rows2 = rows2.transpose(1, 0, 2)
    packed = pl.pallas_call(
        pack_kernel,
        out_shape=jax.ShapeDtypeStruct((half_count, 2, width, blk), BF),
        in_specs=[vmem(), vmem()],
        out_specs=vmem(),
        compiler_params=params(),
    )(by_half(feat_t, other_t), rows2)
    halo = lax.all_to_all(
        packed, "dom", split_axis=0, concat_axis=0, tiled=True, axis_index_groups=groups
    ).reshape(doms, width, blk)

    src = remote_src[0]
    slots = ((src // 16) * pair + src % pair) * 2 + (src // pair) % 2
    tiles = remote_adj.reshape(np_rows, span)
    deg = jnp.broadcast_to(degree.astype(F32)[:, None], (np_rows, width))
    gathered_feat = lax.all_gather(features, "feat", axis=0)
    aggregate = pl.pallas_call(
        agg_kernel,
        out_shape=jax.ShapeDtypeStruct((np_rows, width), BF),
        in_specs=[smem()] + [vmem()] * 5,
        out_specs=vmem(),
        scratch_shapes=[pltpu.VMEM((width, span), BF)],
        compiler_params=params(),
    )(slots, local_adj, features, tiles, halo, deg)
    gathered_agg = lax.all_gather(aggregate, "feat", axis=0)

    full = width * feats
    w_pair = weights.reshape(2, feats, width, width)
    preact = jnp.einsum(
        "krf,kfc->rc", gathered_feat, w_pair[0], preferred_element_type=F32
    ) + jnp.einsum("krf,kfc->rc", gathered_agg, w_pair[1], preferred_element_type=F32)
    output = jax.nn.silu(preact).astype(BF)
    sig = jax.nn.sigmoid(preact)
    grad_pre = (cotangent.astype(F32) * sig * (1.0 + preact * (1.0 - sig))).astype(BF)
    scaled = (grad_pre.astype(F32) / deg).astype(BF)
    scaled_t = scaled.T

    back = pl.pallas_call(
        back_kernel,
        out_shape=jax.ShapeDtypeStruct((doms, width, blk), BF),
        in_specs=[smem(), vmem(), vmem()],
        out_specs=vmem(),
        compiler_params=params(),
    )(slots, scaled_t, tiles).reshape(half_count, 2, width, blk)
    arrived = lax.all_to_all(
        back, "dom", split_axis=0, concat_axis=0, tiled=True, axis_index_groups=groups
    )
    own_term, other_term = pl.pallas_call(
        unpack_kernel,
        out_shape=(
            jax.ShapeDtypeStruct((width, np_rows), F32),
            jax.ShapeDtypeStruct((width, np_rows), BF),
        ),
        in_specs=[vmem()] * 4 + [smem()],
        out_specs=(vmem(), vmem()),
        scratch_shapes=[pltpu.VMEM((2, width, np_rows), F32)],
        compiler_params=params(),
    )(rows2, arrived, scaled_t, local_adj, half.reshape(1).astype(jnp.int32))
    from_other = lax.ppermute(other_term, "dom", swaps)
    neigh_t = (own_term + from_other.astype(F32)).astype(BF)

    terms = jnp.einsum(
        "rf,kcf->krc", grad_pre, w_pair[0], preferred_element_type=F32
    ) + jnp.einsum("fr,kcf->krc", neigh_t, w_pair[1], preferred_element_type=F32)
    landed = lax.all_to_all(terms.astype(BF), "feat", split_axis=0, concat_axis=0, tiled=True)
    grad_input = jnp.sum(landed.astype(F32), axis=0).astype(BF)

    def weight_terms(left):
        return jnp.einsum("krf,rc->kfc", left, grad_pre, preferred_element_type=F32)

    share = jnp.stack([weight_terms(gathered_feat), weight_terms(gathered_agg)])
    share = share.astype(BF).reshape(doms, 2 * full // doms, width)
    shares = lax.all_to_all(share, "dom", split_axis=0, concat_axis=0, tiled=True)
    weight_scale = 1.0 / math.sqrt(doms * np_rows)
    grad_weights = jnp.sum(shares.astype(F32), axis=0) * weight_scale
    return (output, grad_input, grad_weights)


def solution(mesh):
    in_specs = (
        P("dom", "feat"),
        P(None, "feat"),
        P("dom", None, None),
        P("dom", None),
        P("dom", None),
        P("dom", None, None),
        P("dom"),
        P("dom", "feat"),
    )
    out_specs = (P("dom", "feat"), P("dom", "feat"), P("dom", "feat"))
    return jax.shard_map(
        per_device, mesh=mesh, in_specs=in_specs, out_specs=out_specs, check_vma=False
    )
```

time: 961 us -> 368 us (0.38)
  waiting for transfers between devices: 797 us -> 244 us
  other arithmetic: 57.3 us -> 3.6 us
  local copies, waits for them, and re-layouts: 48 us -> 10.4 us
  starting transfers between devices: 30.9 us -> 67.1 us
  Pallas kernels: 0 us -> 16.7 us
    reduce_scatter x2 -> x0, waiting for transfers between devices: 601 us -> none  [the longest x1 494 us: per_device(): lax.psum_scatter(lax.dot_general(combined, grad_pre, (((0,), (0,)), ((),...]
    scatter-add x1 -> x0, other arithmetic: 44.3 us -> none  [per_device(): neigh_grad.at[target_rows]]
    ppermute x0 -> x3, starting transfers between devices: none -> 29.7 us  [the longest x1 15.7 us: per_device(): rows_other = lax.ppermute(rows_own, 'dom', swaps)]
    gather x2 -> x0, local copies, waits for them, and re-layouts: 26.5 us -> none  [the longest x1 22.8 us: per_device(): features[safe_rows]]
    ppermute x0 -> x3, waiting for transfers between devices: none -> 25.1 us  [the longest x1 12.9 us: per_device(): other_t = lax.ppermute(feat_t, 'dom', swaps)]
    pallas_call x0 -> x4, Pallas kernels: none -> 16.7 us  [the longest x1 6.15 us: per_device(): pl.pallas_call(pack_kernel, out_shape=jax.ShapeDtypeStruct((half_count, 2...]
    all_to_all x2 -> x4, waiting for transfers between devices: 77.6 us -> 90.5 us  [the longest x1 48.4 us: per_device(): lax.all_to_all(terms.astype(BF), 'feat', split_axis=0, concat_axis=0, til...]
    all_gather x1 -> x2, waiting for transfers between devices: 118 us -> 128 us  [the longest x1 67 us: per_device(): gathered_agg = lax.all_gather(aggregate, 'feat', axis=0)]
  transfers between devices with their start and end apart: 5 -> 9, of which waited for: 5 -> 7; matrix products, arithmetic and copies ran while one was open for 6% -> 5% of each run, Pallas kernels for 0% -> 2%
where the time goes in v1:
time: 368 us; the launch traced here: 367 us
  waiting for transfers between devices  244 us (66%)
  starting transfers between devices  67.1 us (18%)
  Pallas kernels  16.7 us (5%)
  between operations  14.3 us (4%)
  local copies, waits for them, and re-layouts  10.4 us (3%)
  matrix products  10.3 us (3%)
    all_gather x1, waiting for transfers between devices, per_device(): gathered_agg = lax.all_gather(aggregate, 'feat', axis=0)  67 us
    all_gather x1, waiting for transfers between devices, per_device(): gathered_feat = lax.all_gather(features, 'feat', axis=0)  61 us
    all_to_all x1, waiting for transfers between devices, per_device(): lax.all_to_all(terms.astype(BF), 'feat', split_axis=0, concat_axis=0, til...  48.4 us
    all_to_all x1, waiting for transfers between devices, per_device(): lax.all_to_all(packed, 'dom', split_axis=0, concat_axis=0, tiled=True, ax...  23.2 us
    all_to_all x1, waiting for transfers between devices, per_device(): lax.all_to_all(back, 'dom', split_axis=0, concat_axis=0, tiled=True, axis...  18.9 us
    ppermute x1, starting transfers between devices, per_device(): rows_other = lax.ppermute(rows_own, 'dom', swaps)  15.7 us
    ppermute x1, waiting for transfers between devices, per_device(): other_t = lax.ppermute(feat_t, 'dom', swaps)  12.9 us
    ppermute x1, waiting for transfers between devices, per_device(): from_other = lax.ppermute(other_term, 'dom', swaps)  12.2 us
  transfers between devices with their start and end apart: 9, of which 7 were waited for; matrix products, arithmetic and copies ran while one was open for 5% of the time, Pallas kernels for 2%

profile of v1, /device:TPU:6, one launch (start us, length us, event | category | flops | bytes accessed | tf_op | source)
XLA Modules:
  0.0 366.7 jit_solution(2831069720536451169)
XLA Ops:
  7.2 15.7 %collective-permute-start.1 = (s32[64,128]{1,0:T(8,128)}, s32[64,128]{1,0:T(8,128)S(1)}, u32[]{:S(2)}, u32[]{:S(2)}) collective-permute-start(s32[64,128]{1,0:T(8,128)} %bitcast.98), channel_id=1, source_target_pairs={{0,64},{8,72},{16,80},{24,88},{32,96},{40,104},{48,112},{56,120},{... | collective-permute-start | bytes 98312 | tf_op jit(solution)/shard_map/ppermute | solution.py:115
  23.9 1.9 collective-permute-start
  26.8 12.9 %collective-permute-done = bf16[128,512]{1,0:T(8,128)(2,1)S(1)} collective-permute-done((bf16[128,512]{1,0:T(8,128)(2,1)S(1)}, bf16[128,512]{1,0:T(8,128)(2,1)S(1)}, u32[]{:S(2)}, u32[]{:S(2)}) %collective-permute-start) | collective-permute-done | bytes 131104 | tf_op jit(solution)/shard_map/ppermute | solution.py:113
  39.8 6.2 %shard_map.103 = bf16[32,2,128,128]{3,2,1,0:T(8,128)(2,1)} custom-call(bf16[2,128,512]{2,1,0:T(8,128)(2,1)S(1)} %maximum_select_fusion.ft_ref, s32[32,2,128]{2,1,0:T(2,128)S(1)} %bitcast.81), custom_call_target="tpu_custom_call" | custom-call | tf_op jit(solution)/shard_map/pallas_call | solution.py:123
  45.9 7.6 %all-to-all-start = ((bf16[32,2,128,128]{3,2,1,0:T(8,128)(2,1)}), bf16[32,2,128,128]{3,2,1,0:T(8,128)(2,1)}, u32[]{:S(2)}, u32[]{:S(2)}) async-start(bf16[32,2,128,128]{3,2,1,0:T(8,128)(2,1)} %shard_map.103), calls=%async_computation | async-start | bytes 4194304 | tf_op jit(solution)/shard_map/all_to_all | solution.py:130
  53.7 2.2 copy.41
  55.9 23.2 %all-to-all-done = bf16[32,2,128,128]{3,2,1,0:T(8,128)(2,1)} async-done(((bf16[32,2,128,128]{3,2,1,0:T(8,128)(2,1)}), bf16[32,2,128,128]{3,2,1,0:T(8,128)(2,1)}, u32[]{:S(2)}, u32[]{:S(2)}) %all-to-all-start) | async-done | bytes 2097184 | tf_op jit(solution)/shard_map/all_to_all | solution.py:130
  79.3 3.7 %shard_map.104 = bf16[512,128]{1,0:T(8,128)(2,1)} custom-call(s32[64]{0:T(128)S(1)} %fusion.10.src_ref, bf16[512,512]{1,0:T(8,128)(2,1)S(1)} %copy-done.1, bf16[512,128]{1,0:T(8,128)(2,1)S(1)} %copy-done.2, bf16[512,2048]{1,0:T(8,128)(2,1)S(1)} %bitcast.78, bf16[64,128,128]{2,1,0:T(8,128)(2,1)} %bitcast.13.halo_ref, f32[512,128]{1,0:T(8,128)S(1)} %broadcast_in_dim.2.clone.deg_ref), custom_call_target="tpu_custom_call" | custom-call | tf_op jit(solution)/shard_map/pallas_call | solution.py:139
  85.6 67.0 %all-gather.7.cloned.1.call-done = bf16[4096,128]{1,0:T(8,128)(2,1)} async-done(((bf16[512,128]{1,0:T(8,128)(2,1)}), bf16[4096,128]{1,0:T(8,128)(2,1)}) %all-gather.7.cloned.1.call-update) | async-done | bytes 1048592 | tf_op jit(solution)/shard_map/all_gather | solution.py:147
  152.6 2.4 convolution_bitcast_fusion
  155.0 61.0 %all-gather.5.cloned.1.call-done = bf16[4096,128]{1,0:T(8,128)(2,1)} async-done(((bf16[512,128]{1,0:T(8,128)(2,1)}), bf16[4096,128]{1,0:T(8,128)(2,1)}) %all-gather.5.cloned.1.call-update) | async-done | bytes 1048592 | tf_op jit(solution)/shard_map/all_gather | solution.py:138
  215.9 2.6 fusion.3
  221.1 7.4 %all-to-all-start.1 = ((bf16[32,2,128,128]{3,2,1,0:T(8,128)(2,1)}), bf16[32,2,128,128]{3,2,1,0:T(8,128)(2,1)S(1)}, u32[]{:S(2)}, u32[]{:S(2)}) async-start(bf16[32,2,128,128]{3,2,1,0:T(8,128)(2,1)} %bitcast.80), calls=%async_computation.1 | async-start | bytes 4194304 | tf_op jit(solution)/shard_map/all_to_all | solution.py:167
  228.5 2.3 copy.23
  230.8 1.7 fusion.1
  232.5 1.7 fusion.13
  235.1 18.9 %all-to-all-done.1.arrived_ref = bf16[32,2,128,128]{3,2,1,0:T(8,128)(2,1)S(1)} async-done(((bf16[32,2,128,128]{3,2,1,0:T(8,128)(2,1)}), bf16[32,2,128,128]{3,2,1,0:T(8,128)(2,1)S(1)}, u32[]{:S(2)}, u32[]{:S(2)}) %all-to-all-start.1) | async-done | bytes 2097184 | tf_op jit(solution)/shard_map/all_to_all | solution.py:167
  254.0 11.5 %all-to-all-start.3 = ((bf16[64,32,128]{2,1,0:T(8,128)(2,1)}), bf16[64,32,128]{2,1,0:T(8,128)(2,1)}, u32[]{:S(2)}, u32[]{:S(2)}) async-start(bf16[64,32,128]{2,1,0:T(8,128)(2,1)} %bitcast.89), calls=%async_computation.3 | async-start | bytes 1048576 | tf_op jit(solution)/shard_map/all_to_all | solution.py:195
  265.5 5.6 %shard_map.106 = (f32[128,512]{1,0:T(8,128)S(1)}, bf16[128,512]{1,0:T(8,128)(2,1)S(1)}) custom-call(s32[32,2,128]{2,1,0:T(2,128)S(1)} %bitcast.82, bf16[32,2,128,128]{3,2,1,0:T(8,128)(2,1)S(1)} %all-to-all-done.1.arrived_ref, bf16[128,512]{1,0:T(8,128)(2,1)S(1)} %get-tuple-element.10.scaled_t_ref, bf16[512,512]{1,0:T(8,128)(2,1)S(1)} %copy-done.1, ...), custom_call_target="tpu_custom_call" | custom-call | tf_op jit(solution)/shard_map/pallas_call | solution.py:170
  271.2 12.1 %collective-permute-start.2 = (bf16[128,512]{1,0:T(8,128)(2,1)S(1)}, bf16[128,512]{1,0:T(8,128)(2,1)S(1)}, u32[]{:S(2)}, u32[]{:S(2)}) collective-permute-start(bf16[128,512]{1,0:T(8,128)(2,1)S(1)} %get-tuple-element.6), channel_id=1, source_target_pairs={{0,64},{8,72},{16,80},{24,88},{32,96},{40,104},{48,112},{56,120},{... | collective-permute-start | bytes 393224 | tf_op jit(solution)/shard_map/ppermute | solution.py:181
  283.7 12.2 %collective-permute-done.2 = bf16[128,512]{1,0:T(8,128)(2,1)S(1)} collective-permute-done((bf16[128,512]{1,0:T(8,128)(2,1)S(1)}, bf16[128,512]{1,0:T(8,128)(2,1)S(1)}, u32[]{:S(2)}, u32[]{:S(2)}) %collective-permute-start.2) | collective-permute-done | bytes 131104 | tf_op jit(solution)/shard_map/ppermute | solution.py:181
  295.9 1.5 fusion
  297.4 10.8 %all-to-all-start.2 = ((bf16[8,512,128]{2,1,0:T(8,128)(2,1)}), bf16[8,512,128]{2,1,0:T(8,128)(2,1)S(1)}, u32[]{:S(2)}, u32[]{:S(2)}) async-start(bf16[8,512,128]{2,1,0:T(8,128)(2,1)} %fusion), calls=%async_computation.2 | async-start | bytes 2097152 | tf_op jit(solution)/shard_map/all_to_all | solution.py:187
  310.7 48.4 %all-to-all-done.2 = bf16[8,512,128]{2,1,0:T(8,128)(2,1)S(1)} async-done(((bf16[8,512,128]{2,1,0:T(8,128)(2,1)}), bf16[8,512,128]{2,1,0:T(8,128)(2,1)S(1)}, u32[]{:S(2)}, u32[]{:S(2)}) %all-to-all-start.2) | async-done | bytes 1048608 | tf_op jit(solution)/shard_map/all_to_all | solution.py:187
  (39 shorter events, 12.0 us)
Async XLA Ops:
  7.2 19.5 %collective-permute-start.1 = (s32[64,128]{1,0:T(8,128)}, s32[64,128]{1,0:T(8,128)S(1)}, u32[]{:S(2)}, u32[]{:S(2)}) collective-permute-start(s32[64,128]{1,0:T(8,128)} %bitcast.98), channel_id=1, source_target_pairs={{0,64},{8,72},{16,80},{24,88},{32,96},{40,104},{48,112},{56,120},{... | collective-permute-start | bytes 98312 | tf_op jit(solution)/shard_map/ppermute | solution.py:115
  23.9 15.9 %collective-permute-start = (bf16[128,512]{1,0:T(8,128)(2,1)S(1)}, bf16[128,512]{1,0:T(8,128)(2,1)S(1)}, u32[]{:S(2)}, u32[]{:S(2)}) collective-permute-start(bf16[128,512]{1,0:T(8,128)(2,1)S(1)} %bitcast.95), channel_id=1, source_target_pairs={{0,64},{8,72},{16,80},{24,88},{32,96},{40,104},{48,112},{56,120},{... | collective-permute-start | bytes 393224 | tf_op jit(solution)/shard_map/ppermute | solution.py:113
  45.9 33.2 %all-to-all-start = ((bf16[32,2,128,128]{3,2,1,0:T(8,128)(2,1)}), bf16[32,2,128,128]{3,2,1,0:T(8,128)(2,1)}, u32[]{:S(2)}, u32[]{:S(2)}) async-start(bf16[32,2,128,128]{3,2,1,0:T(8,128)(2,1)} %shard_map.103), calls=%async_computation | async-start | bytes 4194304 | tf_op jit(solution)/shard_map/all_to_all | solution.py:130
  53.6 99.0 %all-gather.7.cloned.1.call-start = ((), (), s32[]{:S(2)}) async-start(), calls=%async_computation.5 | async-start | bytes 1179648 | tf_op jit(solution)/shard_map/all_gather | solution.py:147
  53.6 2.3 copy-start.5
  53.6 2.3 copy-start.6
  53.6 25.6 %copy-start.1 = (bf16[512,512]{1,0:T(8,128)(2,1)S(1)}, bf16[512,512]{1,0:T(8,128)(2,1)}, u32[]{:S(2)}) copy-start(bf16[512,512]{1,0:T(8,128)(2,1)} %local_ref.3) | copy-start | bytes 1572868
  53.7 25.6 %copy-start.2 = (bf16[512,128]{1,0:T(8,128)(2,1)S(1)}, bf16[512,128]{1,0:T(8,128)(2,1)}, u32[]{:S(2)}) copy-start(bf16[512,128]{1,0:T(8,128)(2,1)} %feat_ref.1) | copy-start | bytes 393220
  79.3 4.5 %copy-start.3 = (bf16[512,128]{1,0:T(8,128)(2,1)S(1)}, bf16[512,128]{1,0:T(8,128)(2,1)}, u32[]{:S(2)}) copy-start(bf16[512,128]{1,0:T(8,128)(2,1)} %param.15) | copy-start | bytes 393220
  83.0 132.9 %all-gather.5.cloned.1.call-start = ((), (), s32[]{:S(2)}) async-start(), calls=%async_computation.4 | async-start | bytes 1179648 | tf_op jit(solution)/shard_map/all_gather | solution.py:138
  219.8 1.3 copy-start
  221.1 32.8 %all-to-all-start.1 = ((bf16[32,2,128,128]{3,2,1,0:T(8,128)(2,1)}), bf16[32,2,128,128]{3,2,1,0:T(8,128)(2,1)S(1)}, u32[]{:S(2)}, u32[]{:S(2)}) async-start(bf16[32,2,128,128]{3,2,1,0:T(8,128)(2,1)} %bitcast.80), calls=%async_computation.1 | async-start | bytes 4194304 | tf_op jit(solution)/shard_map/all_to_all | solution.py:167
  254.0 43.4 %all-to-all-start.3 = ((bf16[64,32,128]{2,1,0:T(8,128)(2,1)}), bf16[64,32,128]{2,1,0:T(8,128)(2,1)}, u32[]{:S(2)}, u32[]{:S(2)}) async-start(bf16[64,32,128]{2,1,0:T(8,128)(2,1)} %bitcast.89), calls=%async_computation.3 | async-start | bytes 1048576 | tf_op jit(solution)/shard_map/all_to_all | solution.py:195
  271.2 24.8 %collective-permute-start.2 = (bf16[128,512]{1,0:T(8,128)(2,1)S(1)}, bf16[128,512]{1,0:T(8,128)(2,1)S(1)}, u32[]{:S(2)}, u32[]{:S(2)}) collective-permute-start(bf16[128,512]{1,0:T(8,128)(2,1)S(1)} %get-tuple-element.6), channel_id=1, source_target_pairs={{0,64},{8,72},{16,80},{24,88},{32,96},{40,104},{48,112},{56,120},{... | collective-permute-start | bytes 393224 | tf_op jit(solution)/shard_map/ppermute | solution.py:181
  295.9 12.3 %copy-start.4 = (bf16[512,128]{0,1:T(8,128)(2,1)S(1)}, bf16[512,128]{0,1:T(8,128)(2,1)}, u32[]{:S(2)}) copy-start(bf16[512,128]{0,1:T(8,128)(2,1)} %get-tuple-element.14) | copy-start | bytes 393220
  297.4 61.7 %all-to-all-start.2 = ((bf16[8,512,128]{2,1,0:T(8,128)(2,1)}), bf16[8,512,128]{2,1,0:T(8,128)(2,1)S(1)}, u32[]{:S(2)}, u32[]{:S(2)}) async-start(bf16[8,512,128]{2,1,0:T(8,128)(2,1)} %fusion), calls=%async_computation.2 | async-start | bytes 2097152 | tf_op jit(solution)/shard_map/all_to_all | solution.py:187
Sparse Core Ops, SparseCore 0:
  83.1 69.4 all-gather.6
  154.7 61.2 all-gather.4

commit v2 on v1

--- a/solution.py
+++ b/solution.py
@@ -10,6 +10,7 @@
 BF = jnp.bfloat16
 F32 = jnp.float32
 VMEM_BYTES = 48 * 1024 * 1024
+PAIR = 8
 NT = (((1,), (1,)), ((), ()))
 
 
@@ -23,6 +24,12 @@
 
 def params():
     return pltpu.CompilerParams(vmem_limit_bytes=VMEM_BYTES)
+
+
+def linked(number):
+    return pltpu.CompilerParams(
+        vmem_limit_bytes=VMEM_BYTES, collective_id=number, has_side_effects=True
+    )
 
 
 def one_hot(rows, count):
@@ -43,7 +50,97 @@
         lax.fori_loop(0, out_ref.shape[0], body, 0, unroll=4)
 
 
-def agg_kernel(src_ref, local_ref, feat_ref, tiles_ref, halo_ref, deg_ref, agg_ref, ordered):
+def enter(partner=None):
+    me = lax.axis_index("feat")
+    feats = lax.axis_size("feat")
+    barrier = pltpu.get_barrier_semaphore()
+    places = [{"feat": lax.rem(me + 1, feats)}, {"feat": lax.rem(me + feats - 1, feats)}]
+    if partner is not None:
+        places.append({"dom": partner})
+    for place in places:
+        pl.semaphore_signal(barrier, inc=1, device_id=place, device_id_type=pl.DeviceIdType.MESH)
+    pl.semaphore_wait(barrier, len(places))
+
+
+class LineGather:
+    def __init__(self, own, blocks, send, recv):
+        self.own, self.blocks, self.send, self.recv = own, blocks, send, recv
+        self.me = lax.axis_index("feat")
+        self.last = lax.axis_size("feat") - 1
+
+    def copy(self, way, step, coming=0):
+        up = way == 0
+        back = step + coming
+        source = jnp.clip(self.me - back if up else self.me + back, 0, self.last)
+        target = jnp.clip(self.me + 1 if up else self.me - 1, 0, self.last)
+        return pltpu.make_async_remote_copy(
+            src_ref=self.own if back == 0 else self.blocks.at[source],
+            dst_ref=self.blocks.at[source],
+            send_sem=self.send.at[way, step],
+            recv_sem=self.recv.at[way, step],
+            device_id={"feat": target},
+            device_id_type=pl.DeviceIdType.MESH,
+        )
+
+    def sends(self, way, step):
+        if way == 0:
+            return jnp.logical_and(self.me >= step, self.me < self.last)
+        return jnp.logical_and(self.me <= self.last - step, self.me > 0)
+
+    def gets(self, way, step):
+        return self.me > step if way == 0 else self.me < self.last - step
+
+    def start(self, step):
+        for way in range(2):
+
+            @pl.when(self.sends(way, step))
+            def _():
+                self.copy(way, step).start()
+
+    def arrive(self, step):
+        for way in range(2):
+
+            @pl.when(self.gets(way, step))
+            def _():
+                self.copy(way, step, 1).wait_recv()
+
+    def finish(self):
+        for step in range(self.last):
+            for way in range(2):
+
+                @pl.when(self.sends(way, step))
+                def _():
+                    self.copy(way, step).wait_send()
+
+
+def run_lines(lines):
+    last = lines[0].last
+    for step in range(last):
+        for line in lines:
+            line.arrive(step)
+            if step + 1 < last:
+                line.start(step + 1)
+    for line in lines:
+        line.finish()
+
+
+def line_scratch(feats, rows, width):
+    return [
+        pltpu.VMEM((feats, rows, width), BF),
+        pltpu.SemaphoreType.DMA((2, feats - 1)),
+        pltpu.SemaphoreType.DMA((2, feats - 1)),
+    ]
+
+
+def agg_kernel(
+    src_ref, local_ref, feat_ref, tiles_ref, halo_ref, deg_ref, all_feat_ref, all_agg_ref,
+    ordered, agg_ref, held_feat, send_feat, recv_feat, held_agg, send_agg, recv_agg,
+):
+    me = lax.axis_index("feat")
+    enter()
+    feat_line = LineGather(feat_ref, held_feat, send_feat, recv_feat)
+    agg_line = LineGather(agg_ref, held_agg, send_agg, recv_agg)
+    feat_line.start(0)
     blk = halo_ref.shape[1]
     blocks = local_ref.shape[0] // blk
     span = tiles_ref.shape[1] // blk
@@ -58,6 +155,13 @@
         return carry
 
     lax.fori_loop(0, blocks, body, 0)
+    agg_line.start(0)
+    held_feat[me] = feat_ref[...]
+    held_agg[me] = agg_ref[...]
+    run_lines([feat_line, agg_line])
+    for k in range(held_feat.shape[0]):
+        all_feat_ref[k] = held_feat[k]
+        all_agg_ref[k] = held_agg[k]
 
 
 def back_kernel(src_ref, scaled_t_ref, tiles_ref, back_ref):
@@ -73,9 +177,20 @@
             back_ref[src_ref[b * span + t]] = terms[:, t * blk:(t + 1) * blk]
 
 
-def unpack_kernel(rows_ref, arrived_ref, scaled_t_ref, local_ref, half_ref, own_ref, other_ref, total):
+def unpack_kernel(
+    rows_ref, arrived_ref, scaled_t_ref, local_ref, grad_ref, all_grad_ref, all_neigh_ref,
+    total, other_ref, landed_ref, neigh_ref, swap_send, swap_recv,
+    held_grad, send_grad, recv_grad, held_neigh, send_neigh, recv_neigh,
+):
+    me = lax.axis_index("feat")
+    dom = lax.axis_index("dom")
     count = local_ref.shape[1]
-    half = half_ref[0]
+    half = lax.rem(dom // PAIR, 2)
+    partner = dom + PAIR * (1 - 2 * half)
+    enter(partner)
+    grad_line = LineGather(grad_ref, held_grad, send_grad, recv_grad)
+    neigh_line = LineGather(neigh_ref, held_neigh, send_neigh, recv_neigh)
+    grad_line.start(0)
     total[...] = jnp.zeros_like(total)
     for z in range(2):
 
@@ -92,9 +207,42 @@
             return carry
 
         lax.fori_loop(0, arrived_ref.shape[0] // 2, body, 0, unroll=2)
+    other_ref[...] = total[1 - half].astype(BF)
+    swap = pltpu.make_async_remote_copy(
+        src_ref=other_ref,
+        dst_ref=landed_ref,
+        send_sem=swap_send,
+        recv_sem=swap_recv,
+        device_id={"dom": partner},
+        device_id_type=pl.DeviceIdType.MESH,
+    )
+    swap.start()
+    held_grad[me] = grad_ref[...]
     local = jnp.dot(scaled_t_ref[...], local_ref[...], preferred_element_type=F32)
-    own_ref[...] = local + total[half]
-    other_ref[...] = total[1 - half].astype(BF)
+    total[half] += local
+    run_first = 2
+    for step in range(run_first):
+        grad_line.arrive(step)
+        grad_line.start(step + 1)
+    swap.wait()
+    neigh = (total[half] + landed_ref[...].astype(F32)).astype(BF)
+    neigh_ref[...] = neigh
+    neigh_line.start(0)
+    held_neigh[me] = neigh
+    last = grad_line.last
+    for step in range(last):
+        if step >= run_first:
+            grad_line.arrive(step)
+            if step + 1 < last:
+                grad_line.start(step + 1)
+        neigh_line.arrive(step)
+        if step + 1 < last:
+            neigh_line.start(step + 1)
+    grad_line.finish()
+    neigh_line.finish()
+    for k in range(held_grad.shape[0]):
+        all_grad_ref[k] = held_grad[k]
+        all_neigh_ref[k] = held_neigh[k]
 
 
 def per_device(features, weights, send_rows, remote_src, local_adj, remote_adj, degree, cotangent):
@@ -104,7 +252,7 @@
     blk = remote_adj.shape[2]
     span = remote_adj.shape[1] * blk
     half_count = doms // 2
-    pair = 8
+    pair = PAIR
     half = (lax.axis_index("dom") // pair) % 2
     swaps = [(d, d ^ pair) for d in range(doms)]
     groups = [[d for d in range(doms) if (d // pair) % 2 == h] for h in range(2)]
@@ -131,23 +279,26 @@
         packed, "dom", split_axis=0, concat_axis=0, tiled=True, axis_index_groups=groups
     ).reshape(doms, width, blk)
 
+    w_pair = weights.reshape(2, feats, width, width)
+    w_rows = lax.all_to_all(
+        w_pair.transpose(1, 0, 2, 3), "feat", split_axis=0, concat_axis=0, tiled=True
+    )
+
     src = remote_src[0]
     slots = ((src // 16) * pair + src % pair) * 2 + (src // pair) % 2
     tiles = remote_adj.reshape(np_rows, span)
     deg = jnp.broadcast_to(degree.astype(F32)[:, None], (np_rows, width))
-    gathered_feat = lax.all_gather(features, "feat", axis=0)
-    aggregate = pl.pallas_call(
+    gathered_feat, gathered_agg = pl.pallas_call(
         agg_kernel,
-        out_shape=jax.ShapeDtypeStruct((np_rows, width), BF),
+        out_shape=(jax.ShapeDtypeStruct((feats, np_rows, width), BF),) * 2,
         in_specs=[smem()] + [vmem()] * 5,
-        out_specs=vmem(),
-        scratch_shapes=[pltpu.VMEM((width, span), BF)],
-        compiler_params=params(),
+        out_specs=(vmem(), vmem()),
+        scratch_shapes=[pltpu.VMEM((width, span), BF), pltpu.VMEM((np_rows, width), BF)]
+        + line_scratch(feats, np_rows, width) * 2,
+        compiler_params=linked(1),
     )(slots, local_adj, features, tiles, halo, deg)
-    gathered_agg = lax.all_gather(aggregate, "feat", axis=0)
 
     full = width * feats
-    w_pair = weights.reshape(2, feats, width, width)
     preact = jnp.einsum(
         "krf,kfc->rc", gathered_feat, w_pair[0], preferred_element_type=F32
     ) + jnp.einsum("krf,kfc->rc", gathered_agg, w_pair[1], preferred_element_type=F32)
@@ -167,25 +318,30 @@
     arrived = lax.all_to_all(
         back, "dom", split_axis=0, concat_axis=0, tiled=True, axis_index_groups=groups
     )
-    own_term, other_term = pl.pallas_call(
+    gathered_grad, gathered_neigh = pl.pallas_call(
         unpack_kernel,
         out_shape=(
-            jax.ShapeDtypeStruct((width, np_rows), F32),
-            jax.ShapeDtypeStruct((width, np_rows), BF),
+            jax.ShapeDtypeStruct((feats, np_rows, width), BF),
+            jax.ShapeDtypeStruct((feats, width, np_rows), BF),
         ),
-        in_specs=[vmem()] * 4 + [smem()],
+        in_specs=[vmem()] * 5,
         out_specs=(vmem(), vmem()),
-        scratch_shapes=[pltpu.VMEM((2, width, np_rows), F32)],
-        compiler_params=params(),
-    )(rows2, arrived, scaled_t, local_adj, half.reshape(1).astype(jnp.int32))
-    from_other = lax.ppermute(other_term, "dom", swaps)
-    neigh_t = (own_term + from_other.astype(F32)).astype(BF)
-
-    terms = jnp.einsum(
-        "rf,kcf->krc", grad_pre, w_pair[0], preferred_element_type=F32
-    ) + jnp.einsum("fr,kcf->krc", neigh_t, w_pair[1], preferred_element_type=F32)
-    landed = lax.all_to_all(terms.astype(BF), "feat", split_axis=0, concat_axis=0, tiled=True)
-    grad_input = jnp.sum(landed.astype(F32), axis=0).astype(BF)
+        scratch_shapes=[
+            pltpu.VMEM((2, width, np_rows), F32),
+            pltpu.VMEM((width, np_rows), BF),
+            pltpu.VMEM((width, np_rows), BF),
+            pltpu.VMEM((width, np_rows), BF),
+            pltpu.SemaphoreType.DMA,
+            pltpu.SemaphoreType.DMA,
+        ]
+        + line_scratch(feats, np_rows, width)
+        + line_scratch(feats, width, np_rows),
+        compiler_params=linked(2),
+    )(rows2, arrived, scaled_t, local_adj, grad_pre)
+    grad_input = (
+        jnp.einsum("krc,kfc->rf", gathered_grad, w_rows[:, 0], preferred_element_type=F32)
+        + jnp.einsum("kcr,kfc->rf", gathered_neigh, w_rows[:, 1], preferred_element_type=F32)
+    ).astype(BF)
 
     def weight_terms(left):
         return jnp.einsum("krf,rc->kfc", left, grad_pre, preferred_element_type=F32)

time: 368 us -> 281 us (0.76)
  waiting for transfers between devices: 244 us -> 59.9 us
  Pallas kernels: 16.7 us -> 146 us
  between operations: 14.3 us -> 0.97 us
  starting transfers between devices: 67.1 us -> 56.6 us
    pallas_call x2, Pallas kernels: 9.32 us -> 139 us  [the longest x1 76 us: per_device(): pl.pallas_call(unpack_kernel, out_shape=(jax.ShapeDtypeStruct((feats, np_...]
    all_gather x2 -> x0, waiting for transfers between devices: 128 us -> none  [the longest x1 67 us: per_device(): gathered_agg = lax.all_gather(aggregate, 'feat', axis=0)]
    all_to_all x1, waiting for transfers between devices: 48.4 us -> 0.01 us  [per_device(): lax.all_to_all(w_pair.transpose(1, 0, 2, 3), 'feat', split_axis=0, concat...]
    ppermute x1 -> x0, waiting for transfers between devices: 12.2 us -> none  [per_device(): from_other = lax.ppermute(other_term, 'dom', swaps)]
    ppermute x1 -> x0, starting transfers between devices: 12.1 us -> none  [per_device(): from_other = lax.ppermute(other_term, 'dom', swaps)]
  transfers between devices with their start and end apart: 9 -> 6, of which waited for: 7 -> 3; matrix products, arithmetic and copies ran while one was open for 5% -> 5% of each run, Pallas kernels for 2% -> 50%
where the time goes in v2:
time: 281 us; the launch traced here: 280 us
  Pallas kernels  146 us (52%)
  waiting for transfers between devices  59.9 us (21%)
  starting transfers between devices  56.6 us (20%)
  local copies, waits for them, and re-layouts  7.44 us (3%)
  matrix products  7.3 us (3%)
    pallas_call x1, Pallas kernels, per_device(): pl.pallas_call(unpack_kernel, out_shape=(jax.ShapeDtypeStruct((feats, np_...  76 us
    pallas_call x1, Pallas kernels, per_device(): pl.pallas_call(agg_kernel, out_shape=(jax.ShapeDtypeStruct((feats, np_row...  62.7 us
    all_to_all x1, waiting for transfers between devices, per_device(): lax.all_to_all(packed, 'dom', split_axis=0, concat_axis=0, tiled=True, ax...  24.6 us
    all_to_all x1, waiting for transfers between devices, per_device(): lax.all_to_all(back, 'dom', split_axis=0, concat_axis=0, tiled=True, axis...  22.4 us
    ppermute x1, starting transfers between devices, per_device(): rows_other = lax.ppermute(rows_own, 'dom', swaps)  15.7 us
    ppermute x1, waiting for transfers between devices, per_device(): other_t = lax.ppermute(feat_t, 'dom', swaps)  12.9 us
    all_to_all x1, starting transfers between devices, per_device(): lax.all_to_all(w_pair.transpose(1, 0, 2, 3), 'feat', split_axis=0, concat...  12.7 us
    all_to_all x1, starting transfers between devices, per_device(): lax.all_to_all(share, 'dom', split_axis=0, concat_axis=0, tiled=True)  11.1 us
  transfers between devices with their start and end apart: 6, of which 3 were waited for; matrix products, arithmetic and copies ran while one was open for 5% of the time, Pallas kernels for 50%

profile of v2, /device:TPU:6, one launch (start us, length us, event | category | flops | bytes accessed | tf_op | source)
XLA Modules:
  0.0 279.9 jit_solution(9449105699267742460)
XLA Ops:
  0.6 15.7 %collective-permute-start.1 = (s32[64,128]{1,0:T(8,128)}, s32[64,128]{1,0:T(8,128)S(1)}, u32[]{:S(2)}, u32[]{:S(2)}) collective-permute-start(s32[64,128]{1,0:T(8,128)} %bitcast.96), channel_id=1, source_target_pairs={{0,64},{8,72},{16,80},{24,88},{32,96},{40,104},{48,112},{56,120},{... | collective-permute-start | bytes 98312 | tf_op jit(solution)/shard_map/ppermute | solution.py:263
  16.4 1.0 copy.33
  17.4 1.9 collective-permute-start
  19.3 0.8 copy.34
  20.3 12.9 %collective-permute-done = bf16[128,512]{1,0:T(8,128)(2,1)S(1)} collective-permute-done((bf16[128,512]{1,0:T(8,128)(2,1)S(1)}, bf16[128,512]{1,0:T(8,128)(2,1)S(1)}, u32[]{:S(2)}, u32[]{:S(2)}) %collective-permute-start) | collective-permute-done | bytes 131104 | tf_op jit(solution)/shard_map/ppermute | solution.py:261
  33.3 6.2 %shard_map.103 = bf16[32,2,128,128]{3,2,1,0:T(8,128)(2,1)} custom-call(bf16[2,128,512]{2,1,0:T(8,128)(2,1)S(1)} %maximum_select_fusion.ft_ref, s32[32,2,128]{2,1,0:T(2,128)S(1)} %bitcast.86), custom_call_target="tpu_custom_call" | custom-call | tf_op jit(solution)/shard_map/pallas_call | solution.py:271
  39.4 7.7 %all-to-all-start = ((bf16[32,2,128,128]{3,2,1,0:T(8,128)(2,1)}), bf16[32,2,128,128]{3,2,1,0:T(8,128)(2,1)S(1)}, u32[]{:S(2)}, u32[]{:S(2)}) async-start(bf16[32,2,128,128]{3,2,1,0:T(8,128)(2,1)} %shard_map.103), calls=%async_computation | async-start | bytes 4194304 | tf_op jit(solution)/shard_map/all_to_all | solution.py:278
  47.1 0.8 copy.40
  48.0 24.6 %all-to-all-done = bf16[32,2,128,128]{3,2,1,0:T(8,128)(2,1)S(1)} async-done(((bf16[32,2,128,128]{3,2,1,0:T(8,128)(2,1)}), bf16[32,2,128,128]{3,2,1,0:T(8,128)(2,1)S(1)}, u32[]{:S(2)}, u32[]{:S(2)}) %all-to-all-start) | async-done | bytes 2097184 | tf_op jit(solution)/shard_map/all_to_all | solution.py:278
  72.6 12.7 %all-to-all-start.2 = ((bf16[8,2,128,128]{3,2,1,0:T(8,128)(2,1)}), bf16[8,2,128,128]{3,2,1,0:T(8,128)(2,1)}, u32[]{:S(2)}, u32[]{:S(2)}) async-start(bf16[8,2,128,128]{3,2,1,0:T(8,128)(2,1)} %copy.40), calls=%async_computation.2 | async-start | bytes 1048576 | tf_op jit(solution)/shard_map/all_to_all | solution.py:283
  85.3 2.2 copy.53
  87.8 62.7 %shard_map.104 = (bf16[8,512,128]{2,1,0:T(8,128)(2,1)S(1)}, bf16[8,512,128]{2,1,0:T(8,128)(2,1)S(1)}) custom-call(s32[64]{0:T(128)S(1)} %fusion.9.src_ref, bf16[512,512]{1,0:T(8,128)(2,1)S(1)} %copy-done.1, bf16[512,128]{1,0:T(8,128)(2,1)S(1)} %copy-done.4, bf16[512,2048]{1,0:T(8,128)(2,1)S(1)} %bitcast.83, bf16[64,128,128]{2,1,0:T(8,128)(2,1)} %bitcast.88, ...), custom_call_target="tpu_custom_call" | custom-call | tf_op jit(solution)/shard_map/pallas_call | solution.py:291
  150.9 1.2 fusion.5
  152.1 1.0 copy.38.scaled_t_ref
  153.1 1.2 shard_map.105
  154.4 1.3 copy-done
  155.7 7.5 %all-to-all-start.1 = ((bf16[32,2,128,128]{3,2,1,0:T(8,128)(2,1)}), bf16[32,2,128,128]{3,2,1,0:T(8,128)(2,1)S(1)}, u32[]{:S(2)}, u32[]{:S(2)}) async-start(bf16[32,2,128,128]{3,2,1,0:T(8,128)(2,1)} %bitcast.85), calls=%async_computation.1 | async-start | bytes 4194304 | tf_op jit(solution)/shard_map/all_to_all | solution.py:318
  163.2 1.7 fusion
  165.4 0.8 pad_maximum_fusion
  166.2 22.4 %all-to-all-done.1.arrived_ref = bf16[32,2,128,128]{3,2,1,0:T(8,128)(2,1)S(1)} async-done(((bf16[32,2,128,128]{3,2,1,0:T(8,128)(2,1)}), bf16[32,2,128,128]{3,2,1,0:T(8,128)(2,1)S(1)}, u32[]{:S(2)}, u32[]{:S(2)}) %all-to-all-start.1) | async-done | bytes 2097184 | tf_op jit(solution)/shard_map/all_to_all | solution.py:318
  188.6 11.1 %all-to-all-start.3 = ((bf16[64,32,128]{2,1,0:T(8,128)(2,1)}), bf16[64,32,128]{2,1,0:T(8,128)(2,1)S(1)}, u32[]{:S(2)}, u32[]{:S(2)}) async-start(bf16[64,32,128]{2,1,0:T(8,128)(2,1)} %bitcast.27), calls=%async_computation.3 | async-start | bytes 1048576 | tf_op jit(solution)/shard_map/all_to_all | solution.py:351
  199.7 76.0 %shard_map.106 = (bf16[8,512,128]{2,1,0:T(8,128)(2,1)S(1)}, bf16[8,128,512]{2,1,0:T(8,128)(2,1)S(1)}) custom-call(s32[32,2,128]{2,1,0:T(2,128)S(1)} %bitcast.87, bf16[32,2,128,128]{3,2,1,0:T(8,128)(2,1)S(1)} %all-to-all-done.1.arrived_ref, bf16[128,512]{1,0:T(8,128)(2,1)S(1)} %copy.38.scaled_t_ref, bf16[512,512]{1,0:T(8,128)(2,1)S(1)} %copy-done.2, ...), custom_call_target="tpu_custom_call" | custom-call | tf_op jit(solution)/shard_map/pallas_call | solution.py:321
  275.8 1.4 convolution_bitcast_fusion
  277.2 2.0 fusion.4
  (36 shorter events, 2.0 us)
Async XLA Ops:
  0.6 19.5 %collective-permute-start.1 = (s32[64,128]{1,0:T(8,128)}, s32[64,128]{1,0:T(8,128)S(1)}, u32[]{:S(2)}, u32[]{:S(2)}) collective-permute-start(s32[64,128]{1,0:T(8,128)} %bitcast.96), channel_id=1, source_target_pairs={{0,64},{8,72},{16,80},{24,88},{32,96},{40,104},{48,112},{56,120},{... | collective-permute-start | bytes 98312 | tf_op jit(solution)/shard_map/ppermute | solution.py:263
  17.4 15.9 %collective-permute-start = (bf16[128,512]{1,0:T(8,128)(2,1)S(1)}, bf16[128,512]{1,0:T(8,128)(2,1)S(1)}, u32[]{:S(2)}, u32[]{:S(2)}) collective-permute-start(bf16[128,512]{1,0:T(8,128)(2,1)S(1)} %bitcast.92), channel_id=1, source_target_pairs={{0,64},{8,72},{16,80},{24,88},{32,96},{40,104},{48,112},{56,120},{... | collective-permute-start | bytes 393224 | tf_op jit(solution)/shard_map/ppermute | solution.py:261
  39.4 7.7 %copy-start.6 = (bf16[2048,128]{1,0:T(8,128)(2,1)S(1)}, bf16[2048,128]{1,0:T(8,128)(2,1)}, u32[]{:S(2)}) copy-start(bf16[2048,128]{1,0:T(8,128)(2,1)} %param.9) | copy-start | bytes 1572868
  39.4 33.1 %all-to-all-start = ((bf16[32,2,128,128]{3,2,1,0:T(8,128)(2,1)}), bf16[32,2,128,128]{3,2,1,0:T(8,128)(2,1)S(1)}, u32[]{:S(2)}, u32[]{:S(2)}) async-start(bf16[32,2,128,128]{3,2,1,0:T(8,128)(2,1)} %shard_map.103), calls=%async_computation | async-start | bytes 4194304 | tf_op jit(solution)/shard_map/all_to_all | solution.py:278
  72.6 12.7 %copy-start.5 = (bf16[32,2,128,128]{3,2,1,0:T(8,128)(2,1)}, bf16[32,2,128,128]{3,2,1,0:T(8,128)(2,1)S(1)}, u32[]{:S(2)}) copy-start(bf16[32,2,128,128]{3,2,1,0:T(8,128)(2,1)S(1)} %all-to-all-done) | copy-start | bytes 6291460
  72.6 83.2 %all-to-all-start.2 = ((bf16[8,2,128,128]{3,2,1,0:T(8,128)(2,1)}), bf16[8,2,128,128]{3,2,1,0:T(8,128)(2,1)}, u32[]{:S(2)}, u32[]{:S(2)}) async-start(bf16[8,2,128,128]{3,2,1,0:T(8,128)(2,1)} %copy.40), calls=%async_computation.2 | async-start | bytes 1048576 | tf_op jit(solution)/shard_map/all_to_all | solution.py:283
  85.2 2.3 copy-start.8
  85.3 2.3 copy-start.10
  85.3 2.3 copy-start.7
  85.3 2.5 copy-start.1
  85.3 2.5 copy-start.4
  87.8 63.1 %copy-start.9 = (bf16[512,128]{1,0:T(8,128)(2,1)S(1)}, bf16[512,128]{1,0:T(8,128)(2,1)}, u32[]{:S(2)}) copy-start(bf16[512,128]{1,0:T(8,128)(2,1)} %param.15) | copy-start | bytes 393220
  150.5 1.7 copy-start.3
  154.4 1.3 copy-start
  155.7 32.9 %all-to-all-start.1 = ((bf16[32,2,128,128]{3,2,1,0:T(8,128)(2,1)}), bf16[32,2,128,128]{3,2,1,0:T(8,128)(2,1)S(1)}, u32[]{:S(2)}, u32[]{:S(2)}) async-start(bf16[32,2,128,128]{3,2,1,0:T(8,128)(2,1)} %bitcast.85), calls=%async_computation.1 | async-start | bytes 4194304 | tf_op jit(solution)/shard_map/all_to_all | solution.py:318
  165.4 34.3 %copy-start.2 = (bf16[512,512]{1,0:T(8,128)(2,1)S(1)}, bf16[512,512]{1,0:T(8,128)(2,1)}, u32[]{:S(2)}) copy-start(bf16[512,512]{1,0:T(8,128)(2,1)} %local_ref.3) | copy-start | bytes 1572868
  188.6 90.6 %all-to-all-start.3 = ((bf16[64,32,128]{2,1,0:T(8,128)(2,1)}), bf16[64,32,128]{2,1,0:T(8,128)(2,1)S(1)}, u32[]{:S(2)}, u32[]{:S(2)}) async-start(bf16[64,32,128]{2,1,0:T(8,128)(2,1)} %bitcast.27), calls=%async_computation.3 | async-start | bytes 1048576 | tf_op jit(solution)/shard_map/all_to_all | solution.py:351

commit v3 on v2

v3 whole, which is shorter than its diff:
```python
import math

import jax
import jax.numpy as jnp
from jax import lax
from jax.experimental import pallas as pl
from jax.experimental.pallas import tpu as pltpu
from jax.sharding import PartitionSpec as P

BF = jnp.bfloat16
F32 = jnp.float32
VMEM_BYTES = 48 * 1024 * 1024
PAIR = 8
NT = (((1,), (1,)), ((), ()))


def vmem():
    return pl.BlockSpec(memory_space=pltpu.VMEM)


def smem():
    return pl.BlockSpec(memory_space=pltpu.SMEM)


def params():
    return pltpu.CompilerParams(vmem_limit_bytes=VMEM_BYTES)


def linked(number):
    return pltpu.CompilerParams(
        vmem_limit_bytes=VMEM_BYTES, collective_id=number, has_side_effects=True
    )


def one_hot(rows, count):
    spots = lax.broadcasted_iota(jnp.int32, (count, rows.shape[1]), 0)
    return jnp.where(spots == rows, 1.0, 0.0).astype(BF)


def signal(place):
    pl.semaphore_signal(
        pltpu.get_barrier_semaphore(), inc=1, device_id=place, device_id_type=pl.DeviceIdType.MESH
    )


class Seat:
    def __init__(self):
        self.dom = lax.axis_index("dom")
        self.mates = lax.axis_size("dom") // 2
        self.half = lax.rem(self.dom // PAIR, 2)
        self.partner = self.dom + PAIR * (1 - 2 * self.half)
        self.place = (self.dom // (2 * PAIR)) * PAIR + lax.rem(self.dom, PAIR)

    def mate(self, step):
        return lax.rem(self.place + step, self.mates)

    def dom_of(self, place):
        return (place // PAIR) * (2 * PAIR) + self.half * PAIR + lax.rem(place, PAIR)

    def enter(self):
        me = lax.axis_index("feat")
        feats = lax.axis_size("feat")
        signal({"feat": lax.rem(me + 1, feats)})
        signal({"feat": lax.rem(me + feats - 1, feats)})
        signal({"dom": self.partner})

        def body(step, carry):
            signal({"dom": self.dom_of(self.mate(step))})
            return carry

        lax.fori_loop(1, self.mates, body, 0)
        pl.semaphore_wait(pltpu.get_barrier_semaphore(), self.mates + 2)

    def swap(self, src, dst, send, recv):
        return pltpu.make_async_remote_copy(
            src_ref=src, dst_ref=dst, send_sem=send, recv_sem=recv,
            device_id={"dom": self.partner}, device_id_type=pl.DeviceIdType.MESH,
        )

    def mail(self, src, dst, send, recv, place):
        return pltpu.make_async_remote_copy(
            src_ref=src, dst_ref=dst, send_sem=send, recv_sem=recv,
            device_id={"dom": self.dom_of(place)}, device_id_type=pl.DeviceIdType.MESH,
        )

    def for_mates(self, act):
        def body(step, carry):
            act(step, self.mate(step))
            return carry

        lax.fori_loop(1, self.mates, body, 0)


class LineGather:
    def __init__(self, own, blocks, send, recv):
        self.own, self.blocks, self.send, self.recv = own, blocks, send, recv
        self.me = lax.axis_index("feat")
        self.last = lax.axis_size("feat") - 1

    def copy(self, way, step, coming=0):
        up = way == 0
        back = step + coming
        source = jnp.clip(self.me - back if up else self.me + back, 0, self.last)
        target = jnp.clip(self.me + 1 if up else self.me - 1, 0, self.last)
        return pltpu.make_async_remote_copy(
            src_ref=self.own if back == 0 else self.blocks.at[source],
            dst_ref=self.blocks.at[source],
            send_sem=self.send.at[way, step],
            recv_sem=self.recv.at[way, step],
            device_id={"feat": target},
            device_id_type=pl.DeviceIdType.MESH,
        )

    def sends(self, way, step):
        if way == 0:
            return jnp.logical_and(self.me >= step, self.me < self.last)
        return jnp.logical_and(self.me <= self.last - step, self.me > 0)

    def gets(self, way, step):
        return self.me > step if way == 0 else self.me < self.last - step

    def start(self, step):
        for way in range(2):

            @pl.when(self.sends(way, step))
            def _():
                self.copy(way, step).start()

    def arrive(self, step):
        for way in range(2):

            @pl.when(self.gets(way, step))
            def _():
                self.copy(way, step, 1).wait_recv()

    def finish(self):
        for step in range(self.last):
            for way in range(2):

                @pl.when(self.sends(way, step))
                def _():
                    self.copy(way, step).wait_send()


def run_lines(lines):
    last = lines[0].last
    for step in range(last):
        for line in lines:
            line.arrive(step)
            if step + 1 < last:
                line.start(step + 1)
    for line in lines:
        line.finish()


def line_scratch(feats, rows, width):
    return [
        pltpu.VMEM((feats, rows, width), BF),
        pltpu.SemaphoreType.DMA((2, feats - 1)),
        pltpu.SemaphoreType.DMA((2, feats - 1)),
    ]


def forward_kernel(
    src_ref, local_ref, feat_ref, feat_t_ref, rows_ref, tiles_ref, deg_ref,
    all_feat_ref, all_agg_ref, rows_other_ref,
    ordered, agg_ref, halo_ref, packed, other_t, rows_in, swap_send, swap_recv, mail_send, mail_recv,
    held_feat, send_feat, recv_feat, held_agg, send_agg, recv_agg,
):
    me = lax.axis_index("feat")
    seat = Seat()
    half, place = seat.half, seat.place
    count = feat_t_ref.shape[1]
    blk = halo_ref.shape[1]
    blocks = local_ref.shape[0] // blk
    span = tiles_ref.shape[1] // blk
    seat.enter()
    rows_swap = seat.swap(rows_ref.at[1 - half], rows_in, swap_send.at[0], swap_recv.at[0])
    feat_swap = seat.swap(feat_t_ref, other_t, swap_send.at[1], swap_recv.at[1])
    rows_swap.start()
    feat_swap.start()
    feat_line = LineGather(feat_ref, held_feat, send_feat, recv_feat)
    agg_line = LineGather(agg_ref, held_agg, send_agg, recv_agg)
    feat_line.start(0)

    def mail(turn, step, to, sender):
        z = half if turn == 0 else 1 - half
        return seat.mail(
            packed.at[turn, step], halo_ref.at[2 * sender + z],
            mail_send.at[turn, step], mail_recv.at[z, sender], to,
        )

    def picked(turn, to):
        left = feat_t_ref[...] if turn == 0 else other_t[...]
        wanted = rows_ref[half, pl.ds(to, 1), :] if turn == 0 else rows_in[pl.ds(to, 1), :]
        return jnp.dot(left, one_hot(wanted, count), preferred_element_type=F32).astype(BF)

    def post(turn):
        def act(step, to):
            packed[turn, step] = picked(turn, to)
            mail(turn, step, to, place).start()

        seat.for_mates(act)
        halo_ref[2 * place + (half if turn == 0 else 1 - half)] = picked(turn, place)

    post(0)
    feat_line.arrive(0)
    feat_line.start(1)
    rows_swap.wait()
    feat_swap.wait()
    post(1)
    held_feat[me] = feat_ref[...]
    rows_other_ref[...] = rows_in[...]
    for step in range(1, feat_line.last):
        feat_line.arrive(step)
        if step + 1 < feat_line.last:
            feat_line.start(step + 1)
    for turn in range(2):
        seat.for_mates(lambda step, to: mail(turn, step, to, to).wait_recv())

    def body(b, carry):
        for t in range(span):
            ordered[:, t * blk:(t + 1) * blk] = halo_ref[src_ref[b * span + t]]
        rows = pl.ds(pl.multiple_of(b * blk, blk), blk)
        sums = lax.dot_general(tiles_ref[rows, :], ordered[...], NT, preferred_element_type=F32)
        sums += jnp.dot(local_ref[rows, :], feat_ref[...], preferred_element_type=F32)
        agg_ref[rows, :] = (sums / deg_ref[rows, :]).astype(BF)
        return carry

    lax.fori_loop(0, blocks, body, 0)
    agg_line.start(0)
    held_agg[me] = agg_ref[...]
    for k in range(held_feat.shape[0]):
        all_feat_ref[k] = held_feat[k]
    run_lines([agg_line])
    feat_line.finish()
    for turn in range(2):
        seat.for_mates(lambda step, to: mail(turn, step, to, place).wait_send())
    for k in range(held_agg.shape[0]):
        all_agg_ref[k] = held_agg[k]


def back_kernel(src_ref, scaled_t_ref, tiles_ref, back_ref):
    blk = back_ref.shape[1]
    blocks = scaled_t_ref.shape[1] // blk
    span = tiles_ref.shape[1] // blk
    for b in range(blocks):
        left = scaled_t_ref[:, b * blk:(b + 1) * blk]
        terms = jnp.dot(
            left, tiles_ref[b * blk:(b + 1) * blk, :], preferred_element_type=F32
        ).astype(BF)
        for t in range(span):
            back_ref[src_ref[b * span + t]] = terms[:, t * blk:(t + 1) * blk]


def backward_kernel(
    rows_ref, rows_other_ref, back_ref, scaled_t_ref, local_ref, grad_t_ref, w_ref, share_ref,
    grad_in_ref, grad_w_ref,
    arrived, shares, w_mine, w_in, total, other_ref, landed_ref, neigh_ref, terms, came, went,
    swap_send, swap_recv, mail_send, mail_recv, line_send, line_recv,
):
    me = lax.axis_index("feat")
    last = lax.axis_size("feat") - 1
    seat = Seat()
    half, place = seat.half, seat.place
    count = local_ref.shape[1]
    seat.enter()

    def mail(turn, step, to, sender):
        if turn == 2:
            return seat.mail(
                share_ref.at[to], shares.at[sender],
                mail_send.at[2, step], mail_recv.at[2, sender], to,
            )
        z = 1 - half if turn == 0 else half
        return seat.mail(
            back_ref.at[2 * to + z], arrived.at[2 * sender + z],
            mail_send.at[turn, step], mail_recv.at[turn, sender], to,
        )

    for turn in range(3):
        seat.for_mates(lambda step, to: mail(turn, step, to, place).start())
    arrived[2 * place] = back_ref[2 * place]
    arrived[2 * place + 1] = back_ref[2 * place + 1]
    shares[place] = share_ref[place]
    for k in range(last + 1):
        terms[k] = jnp.dot(w_ref[0, k], grad_t_ref[...], preferred_element_type=F32)

    def unpack(turn):
        z = 1 - half if turn == 0 else half
        seat.for_mates(lambda step, to: mail(turn, step, to, to).wait_recv())

        def rows(j):
            return rows_ref[half, pl.ds(j, 1), :] if turn == 1 else rows_other_ref[pl.ds(j, 1), :]

        def body(i, carry):
            j = 2 * i
            left = jnp.concatenate([arrived[2 * j + z], arrived[2 * j + 2 + z]], axis=1)
            right = jnp.concatenate(
                [one_hot(rows(j), count), one_hot(rows(j + 1), count)], axis=1
            )
            total[...] += lax.dot_general(left, right, NT, preferred_element_type=F32)
            return carry

        lax.fori_loop(0, seat.mates // 2, body, 0, unroll=2)

    total[...] = jnp.zeros_like(total)
    unpack(0)
    other_ref[...] = total[...].astype(BF)
    swap = seat.swap(other_ref, landed_ref, swap_send.at[0], swap_recv.at[0])
    swap.start()
    total[...] = jnp.dot(scaled_t_ref[...], local_ref[...], preferred_element_type=F32)
    unpack(1)
    swap.wait()
    neigh_ref[...] = (total[...] + landed_ref[...].astype(F32)).astype(BF)

    def hop(way, tick):
        target = jnp.clip(me + 1 if way == 0 else me - 1, 0, last)
        return pltpu.make_async_remote_copy(
            src_ref=went.at[way, tick], dst_ref=came.at[way, tick],
            send_sem=line_send.at[way, tick], recv_sem=line_recv.at[way, tick],
            device_id={"feat": target}, device_id_type=pl.DeviceIdType.MESH,
        )

    def rank(way):
        return me if way == 0 else last - me

    def term(k):
        return terms[k] + jnp.dot(w_ref[1, k], neigh_ref[...], preferred_element_type=F32)

    def sends(way, tick):
        return jnp.logical_and(rank(way) <= tick, rank(way) < last)

    for tick in range(last):
        for way in range(2):
            k = jnp.clip(last - tick + me if way == 0 else tick - last + me, 0, last)

            if tick > 0:

                @pl.when(jnp.logical_and(rank(way) <= tick, rank(way) > 0))
                def _():
                    hop(way, tick - 1).wait_recv()

                @pl.when(jnp.logical_and(sends(way, tick), rank(way) > 0))
                def _():
                    went[way, tick] = (term(k) + came[way, tick - 1].astype(F32)).astype(BF)

            @pl.when(rank(way) == 0)
            def _():
                went[way, tick] = term(k).astype(BF)

            @pl.when(sends(way, tick))
            def _():
                hop(way, tick).start()

        if tick == 1:
            seat.for_mates(lambda step, to: mail(2, step, to, to).wait_recv())
            summed = jnp.sum(shares[...].astype(F32), axis=0)
            w_mine[...] = summed.reshape(w_mine.shape)
            w_swap = seat.swap(w_mine.at[1 - half], w_in, swap_send.at[1], swap_recv.at[1])
            w_swap.start()
    total[...] = term(me)
    for way in range(2):

        @pl.when(rank(way) > 0)
        def _():
            hop(way, last - 1).wait_recv()
            total[...] += came[way, last - 1].astype(F32)

    grad_in_ref[...] = total[...].astype(BF)
    w_swap.wait()
    grad_w_ref[...] = w_mine[half] + w_in[...]
    for tick in range(last):
        for way in range(2):

            @pl.when(sends(way, tick))
            def _():
                hop(way, tick).wait_send()

    for turn in range(3):
        seat.for_mates(lambda step, to: mail(turn, step, to, place).wait_send())


def per_device(features, weights, send_rows, remote_src, local_adj, remote_adj, degree, cotangent):
    np_rows, width = features.shape
    feats = lax.axis_size("feat")
    doms = lax.axis_size("dom")
    blk = remote_adj.shape[2]
    span = remote_adj.shape[1] * blk
    mates = doms // 2
    rows = send_rows[0].reshape(doms // (2 * PAIR), 2, PAIR, blk).transpose(1, 0, 2, 3)
    rows = rows.reshape(2, mates, blk)
    w_pair = weights.reshape(2, feats, width, width)

    src = remote_src[0]
    slots = ((src // (2 * PAIR)) * PAIR + src % PAIR) * 2 + (src // PAIR) % 2
    tiles = remote_adj.reshape(np_rows, span)
    deg = jnp.broadcast_to(degree.astype(F32)[:, None], (np_rows, width))
    gathered_feat, gathered_agg, rows_other = pl.pallas_call(
        forward_kernel,
        out_shape=(jax.ShapeDtypeStruct((feats, np_rows, width), BF),) * 2
        + (jax.ShapeDtypeStruct((mates, blk), jnp.int32),),
        in_specs=[smem()] + [vmem()] * 6,
        out_specs=(vmem(), vmem(), vmem()),
        scratch_shapes=[
            pltpu.VMEM((width, span), BF),
            pltpu.VMEM((np_rows, width), BF),
            pltpu.VMEM((doms, width, blk), BF),
            pltpu.VMEM((2, mates, width, blk), BF),
            pltpu.VMEM((width, np_rows), BF),
            pltpu.VMEM((mates, blk), jnp.int32),
            pltpu.SemaphoreType.DMA((2,)),
            pltpu.SemaphoreType.DMA((2,)),
            pltpu.SemaphoreType.DMA((2, mates)),
            pltpu.SemaphoreType.DMA((2, mates)),
        ]
        + line_scratch(feats, np_rows, width) * 2,
        compiler_params=linked(1),
    )(slots, local_adj, features, features.T, rows, tiles, deg)

    full = width * feats
    preact = jnp.einsum(
        "krf,kfc->rc", gathered_feat, w_pair[0], preferred_element_type=F32
    ) + jnp.einsum("krf,kfc->rc", gathered_agg, w_pair[1], preferred_element_type=F32)
    output = jax.nn.silu(preact).astype(BF)
    sig = jax.nn.sigmoid(preact)
    grad_pre = (cotangent.astype(F32) * sig * (1.0 + preact * (1.0 - sig))).astype(BF)
    scaled = (grad_pre.astype(F32) / deg).astype(BF)
    scaled_t = scaled.T

    back = pl.pallas_call(
        back_kernel,
        out_shape=jax.ShapeDtypeStruct((doms, width, blk), BF),
        in_specs=[smem(), vmem(), vmem()],
        out_specs=vmem(),
        compiler_params=params(),
    )(slots, scaled_t, tiles)

    def weight_terms(left):
        return jnp.einsum("krf,rc->kfc", left, grad_pre, preferred_element_type=F32)

    cut = 2 * full // doms
    share = jnp.stack([weight_terms(gathered_feat), weight_terms(gathered_agg)]).astype(BF)
    share = share.reshape(doms // (2 * PAIR), 2, PAIR, cut, width).transpose(0, 2, 1, 3, 4)
    share = share.reshape(mates, 2 * cut, width)
    last = feats - 1
    grad_input_t, summed = pl.pallas_call(
        backward_kernel,
        out_shape=(
            jax.ShapeDtypeStruct((width, np_rows), BF),
            jax.ShapeDtypeStruct((cut, width), F32),
        ),
        in_specs=[vmem()] * 8,
        out_specs=(vmem(), vmem()),
        scratch_shapes=[
            pltpu.VMEM((doms, width, blk), BF),
            pltpu.VMEM((mates, 2 * cut, width), BF),
            pltpu.VMEM((2, cut, width), F32),
            pltpu.VMEM((cut, width), F32),
            pltpu.VMEM((width, np_rows), F32),
            pltpu.VMEM((width, np_rows), BF),
            pltpu.VMEM((width, np_rows), BF),
            pltpu.VMEM((width, np_rows), BF),
            pltpu.VMEM((feats, width, np_rows), F32),
            pltpu.VMEM((2, last, width, np_rows), BF),
            pltpu.VMEM((2, last, width, np_rows), BF),
            pltpu.SemaphoreType.DMA((2,)),
            pltpu.SemaphoreType.DMA((2,)),
            pltpu.SemaphoreType.DMA((3, mates)),
            pltpu.SemaphoreType.DMA((3, mates)),
            pltpu.SemaphoreType.DMA((2, last)),
            pltpu.SemaphoreType.DMA((2, last)),
        ],
        compiler_params=linked(2),
    )(rows, rows_other, back, scaled_t, local_adj, grad_pre.T, w_pair, share)
    weight_scale = 1.0 / math.sqrt(doms * np_rows)
    return (output, grad_input_t.T, summed * weight_scale)


def solution(mesh):
    in_specs = (
        P("dom", "feat"),
        P(None, "feat"),
        P("dom", None, None),
        P("dom", None),
        P("dom", None),
        P("dom", None, None),
        P("dom"),
        P("dom", "feat"),
    )
    out_specs = (P("dom", "feat"), P("dom", "feat"), P("dom", "feat"))
    return jax.shard_map(
        per_device, mesh=mesh, in_specs=in_specs, out_specs=out_specs, check_vma=False
    )
```

time: 281 us -> 191 us (0.68)
  the two profiles are of different devices: /device:TPU:6 before, /device:TPU:48 now
where the time goes in v3:
time: 191 us
  Pallas kernels  173 us (91%)
  local copies, waits for them, and re-layouts  11.4 us (6%)
  matrix products  4.17 us (2%)
    pallas_call x1, Pallas kernels, per_device(): pl.pallas_call(forward_kernel, out_shape=(jax.ShapeDtypeStruct((feats, np...  90 us
    pallas_call x1, Pallas kernels, per_device(): pl.pallas_call(backward_kernel, out_shape=(jax.ShapeDtypeStruct((width, n...  81.9 us
    unnamed x37, local copies, waits for them, and re-layouts  9.53 us

profile of v3, /device:TPU:48, one launch (start us, length us, event | category | flops | bytes accessed | tf_op | source)
XLA Modules:
  0.0 190.8 jit_solution(11335180221008026432)
XLA Ops:
  0.7 2.2 %copy.37 = bf16[64,8,16,128]{3,1,2,0:T(8,128)(2,1)S(1)} copy(bf16[64,8,16,128]{3,2,1,0:T(8,128)(2,1)} %bitcast.71) | data formatting | bytes 4194304
  2.9 0.1 broadcast_in_dim.2.clone.deg_ref
  3.0 0.6 copy.38
  3.6 0.5 fusion.7.src_ref
  4.1 0.8 copy.11
  4.9 1.0 copy-done.1
  6.0 0.9 copy-done.6
  6.9 0.8 copy-done.7
  7.6 0.6 copy-done.9
  8.2 90.0 %shard_map.103 = (bf16[8,512,128]{2,1,0:T(8,128)(2,1)S(1)}, bf16[8,512,128]{2,1,0:T(8,128)(2,1)S(1)}, s32[32,128]{1,0:T(8,128)S(1)}) custom-call(s32[64]{0:T(128)S(1)} %copy-done.9, bf16[512,512]{1,0:T(8,128)(2,1)S(1)} %copy-done.1, bf16[512,128]{1,0:T(8,128)(2,1)S(1)} %copy-done.5, bf16[128,512]{1,0:T(8,128)(2,1)S(1)} %bitcast.67, ...), custom_call_target="tpu_custom_call" | custom-call | tf_op jit(solution)/shard_map/pallas_call | solution.py:399
  98.2 1.0 copy-done.3
  99.2 1.1 fusion.9
  100.3 1.2 convolution_bitcast_fusion
  101.5 0.8 copy.16
  102.2 2.0 %fusion.3 = (bf16[128,512]{1,0:T(8,128)(2,1)S(1)}, bf16[512,128]{0,1:T(8,128)(2,1)S(1)}, bf16[512,128]{0,1:T(8,128)(2,1)S(1)}) fusion(f32[512]{0:T(512)} %copy-done.13, bf16[512,128]{0,1:T(8,128)(2,1)} %copy.16, f32[512,128]{0,1:T(8,128)} %convolution_bitcast_fusion, bf16[8,512,128]{2,1,0:T(8,128)(2,1)} %copy-done.3, bf16[8,128,128]{2,1,0:T(8,128)(2,1)S(1)} %bitcast.74), kind=kOutput, calls=%fused_computation.13 | convolution fusion | flops 135266304 | bytes 2099200 | tf_op jit(solution)/shard_map/krf,kfc->rc/dot_general | solution.py:422
  104.3 0.5 fusion
  104.8 0.5 fusion.1
  105.2 0.1 pad_maximum_fusion
  105.3 0.1 copy.21
  105.4 1.3 shard_map.104.back_ref
  106.7 81.9 %shard_map.105 = (bf16[128,512]{1,0:T(8,128)(2,1)S(1)}, f32[32,128]{1,0:T(8,128)S(1)}) custom-call(s32[2,32,128]{2,1,0:T(8,128)S(1)} %bitcast.69, s32[32,128]{1,0:T(8,128)S(1)} %get-tuple-element.10.rows_other_ref, bf16[64,128,128]{2,1,0:T(8,128)(2,1)S(1)} %shard_map.104.back_ref, bf16[128,512]{1,0:T(8,128)(2,1)S(1)} %get-tuple-element.16.scaled_t_ref, ...), custom_call_target="tpu_custom_call" | custom-call | tf_op jit(solution)/shard_map/pallas_call | solution.py:447
  188.6 0.8 copy.23
  189.4 0.6 broadcast_multiply_fusion
  190.0 0.8 copy.22
  (28 shorter events, 0.1 us)
Async XLA Ops:
  0.6 2.2 %copy-start.14 = (s32[512]{0:T(512)S(1)}, s32[512]{0:T(512)}, u32[]{:S(2)}) copy-start(s32[512]{0:T(512)} %param.14) | copy-start | bytes 6148
  0.6 2.4 %copy-start.12 = (s32[1,64,128]{2,1,0:T(8,128)S(1)}, s32[1,64,128]{2,1,0:T(8,128)}, u32[]{:S(2)}) copy-start(s32[1,64,128]{2,1,0:T(8,128)} %param.10) | copy-start | bytes 98308
  0.7 3.0 %copy-start.15 = (s32[1,64]{1,0:T(1,128)S(1)}, s32[1,64]{1,0:T(1,128)}, u32[]{:S(2)}) copy-start(s32[1,64]{1,0:T(1,128)} %param.11) | copy-start | bytes 772
  0.7 3.5 %copy-start.5 = (bf16[512,128]{1,0:T(8,128)(2,1)S(1)}, bf16[512,128]{1,0:T(8,128)(2,1)}, u32[]{:S(2)}) copy-start(bf16[512,128]{1,0:T(8,128)(2,1)} %feat_ref.1) | copy-start | bytes 393220
  2.9 2.0 %copy-start.13 = (f32[512]{0:T(512)}, f32[512]{0:T(512)S(1)}, u32[]{:S(2)}) copy-start(f32[512]{0:T(512)S(1)} %convert_element_type.23) | copy-start | bytes 6148
  4.9 1.0 copy-start.1
  6.0 0.9 copy-start.6
  6.9 0.8 copy-start.7
  7.6 0.6 copy-start.9
  98.2 1.0 copy-start.3
  99.2 2.3 %copy-start.11 = (bf16[512,128]{1,0:T(8,128)(2,1)S(1)}, bf16[512,128]{1,0:T(8,128)(2,1)}, u32[]{:S(2)}) copy-start(bf16[512,128]{1,0:T(8,128)(2,1)} %param.15) | copy-start | bytes 393220
  102.2 2.0 %copy-start.4 = (bf16[8,512,128]{2,1,0:T(8,128)(2,1)S(1)}, bf16[8,512,128]{2,1,0:T(8,128)(2,1)}, u32[]{:S(2)}) copy-start(bf16[8,512,128]{2,1,0:T(8,128)(2,1)} %copy-done.3) | copy-start | bytes 3145732
  104.7 0.6 copy-start.10
  105.4 1.3 copy-start
  105.4 1.3 copy-start.2
  105.4 1.3 copy-start.8

commit v4 on v3

--- a/solution.py
+++ b/solution.py
@@ -8,6 +8,7 @@
 from jax.sharding import PartitionSpec as P
 
 BF = jnp.bfloat16
+PARTS = 2
 F32 = jnp.float32
 VMEM_BYTES = 48 * 1024 * 1024
 PAIR = 8
@@ -142,22 +143,26 @@
                     self.copy(way, step).wait_send()
 
 
-def run_lines(lines):
-    last = lines[0].last
-    for step in range(last):
-        for line in lines:
-            line.arrive(step)
-            if step + 1 < last:
-                line.start(step + 1)
+def gather_lines(own, held, send, recv):
+    rows = held.shape[2]
+    return [
+        LineGather(own.at[pl.ds(c * rows, rows)], held.at[c], send.at[c], recv.at[c])
+        for c in range(PARTS)
+    ]
+
+
+def hand_on(lines, step):
     for line in lines:
-        line.finish()
+        line.arrive(step)
+        if step + 1 < line.last:
+            line.start(step + 1)
 
 
 def line_scratch(feats, rows, width):
     return [
-        pltpu.VMEM((feats, rows, width), BF),
-        pltpu.SemaphoreType.DMA((2, feats - 1)),
-        pltpu.SemaphoreType.DMA((2, feats - 1)),
+        pltpu.VMEM((PARTS, feats, rows // PARTS, width), BF),
+        pltpu.SemaphoreType.DMA((PARTS, 2, feats - 1)),
+        pltpu.SemaphoreType.DMA((PARTS, 2, feats - 1)),
     ]
 
 
@@ -179,9 +184,11 @@
     feat_swap = seat.swap(feat_t_ref, other_t, swap_send.at[1], swap_recv.at[1])
     rows_swap.start()
     feat_swap.start()
-    feat_line = LineGather(feat_ref, held_feat, send_feat, recv_feat)
-    agg_line = LineGather(agg_ref, held_agg, send_agg, recv_agg)
-    feat_line.start(0)
+    feat_lines = gather_lines(feat_ref, held_feat, send_feat, recv_feat)
+    agg_lines = gather_lines(agg_ref, held_agg, send_agg, recv_agg)
+    last = feat_lines[0].last
+    rows_part = held_feat.shape[2]
+    early = last - 2
 
     def mail(turn, step, to, sender):
         z = half if turn == 0 else 1 - half
@@ -204,17 +211,16 @@
         halo_ref[2 * place + (half if turn == 0 else 1 - half)] = picked(turn, place)
 
     post(0)
-    feat_line.arrive(0)
-    feat_line.start(1)
     rows_swap.wait()
     feat_swap.wait()
+    for line in feat_lines:
+        line.start(0)
     post(1)
-    held_feat[me] = feat_ref[...]
+    for c in range(PARTS):
+        held_feat[c, me] = feat_ref[c * rows_part:(c + 1) * rows_part, :]
     rows_other_ref[...] = rows_in[...]
-    for step in range(1, feat_line.last):
-        feat_line.arrive(step)
-        if step + 1 < feat_line.last:
-            feat_line.start(step + 1)
+    for step in range(early):
+        hand_on(feat_lines, step)
     for turn in range(2):
         seat.for_mates(lambda step, to: mail(turn, step, to, to).wait_recv())
 
@@ -227,17 +233,26 @@
         agg_ref[rows, :] = (sums / deg_ref[rows, :]).astype(BF)
         return carry
 
-    lax.fori_loop(0, blocks, body, 0)
-    agg_line.start(0)
-    held_agg[me] = agg_ref[...]
-    for k in range(held_feat.shape[0]):
-        all_feat_ref[k] = held_feat[k]
-    run_lines([agg_line])
-    feat_line.finish()
+    for c in range(PARTS):
+        lax.fori_loop(c * blocks // PARTS, (c + 1) * blocks // PARTS, body, 0)
+        agg_lines[c].start(0)
+    for c in range(PARTS):
+        held_agg[c, me] = agg_ref[c * rows_part:(c + 1) * rows_part, :]
+    for step in range(early, last):
+        hand_on(feat_lines, step)
+    for step in range(last):
+        hand_on(agg_lines, step)
+        if step == 0:
+            for c in range(PARTS):
+                for k in range(held_feat.shape[1]):
+                    all_feat_ref[k, c * rows_part:(c + 1) * rows_part, :] = held_feat[c, k]
+    for line in feat_lines + agg_lines:
+        line.finish()
     for turn in range(2):
         seat.for_mates(lambda step, to: mail(turn, step, to, place).wait_send())
-    for k in range(held_agg.shape[0]):
-        all_agg_ref[k] = held_agg[k]
+    for c in range(PARTS):
+        for k in range(held_agg.shape[1]):
+            all_agg_ref[k, c * rows_part:(c + 1) * rows_part, :] = held_agg[c, k]
 
 
 def back_kernel(src_ref, scaled_t_ref, tiles_ref, back_ref):
@@ -314,11 +329,13 @@
     swap.wait()
     neigh_ref[...] = (total[...] + landed_ref[...].astype(F32)).astype(BF)
 
-    def hop(way, tick):
+    part = came.shape[4]
+
+    def hop(c, way, tick):
         target = jnp.clip(me + 1 if way == 0 else me - 1, 0, last)
         return pltpu.make_async_remote_copy(
-            src_ref=went.at[way, tick], dst_ref=came.at[way, tick],
-            send_sem=line_send.at[way, tick], recv_sem=line_recv.at[way, tick],
+            src_ref=went.at[c, way, tick], dst_ref=came.at[c, way, tick],
+            send_sem=line_send.at[c, way, tick], recv_sem=line_recv.at[c, way, tick],
             device_id={"feat": target}, device_id_type=pl.DeviceIdType.MESH,
         )
 
@@ -332,26 +349,39 @@
         return jnp.logical_and(rank(way) <= tick, rank(way) < last)
 
     for tick in range(last):
+        blocks = [
+            jnp.clip(last - tick + me if way == 0 else tick - last + me, 0, last)
+            for way in range(2)
+        ]
         for way in range(2):
-            k = jnp.clip(last - tick + me if way == 0 else tick - last + me, 0, last)
-
-            if tick > 0:
-
-                @pl.when(jnp.logical_and(rank(way) <= tick, rank(way) > 0))
-                def _():
-                    hop(way, tick - 1).wait_recv()
-
-                @pl.when(jnp.logical_and(sends(way, tick), rank(way) > 0))
-                def _():
-                    went[way, tick] = (term(k) + came[way, tick - 1].astype(F32)).astype(BF)
-
-            @pl.when(rank(way) == 0)
-            def _():
-                went[way, tick] = term(k).astype(BF)
 
             @pl.when(sends(way, tick))
             def _():
-                hop(way, tick).start()
+                terms[blocks[way]] = term(blocks[way])
+
+        for c in range(PARTS):
+            for way in range(2):
+                lanes = slice(c * part, (c + 1) * part)
+
+                if tick > 0:
+
+                    @pl.when(jnp.logical_and(rank(way) <= tick, rank(way) > 0))
+                    def _():
+                        hop(c, way, tick - 1).wait_recv()
+
+                    @pl.when(jnp.logical_and(sends(way, tick), rank(way) > 0))
+                    def _():
+                        went[c, way, tick] = (
+                            terms[blocks[way], :, lanes] + came[c, way, tick - 1].astype(F32)
+                        ).astype(BF)
+
+                @pl.when(rank(way) == 0)
+                def _():
+                    went[c, way, tick] = terms[blocks[way], :, lanes].astype(BF)
+
+                @pl.when(sends(way, tick))
+                def _():
+                    hop(c, way, tick).start()
 
         if tick == 1:
             seat.for_mates(lambda step, to: mail(2, step, to, to).wait_recv())
@@ -360,22 +390,24 @@
             w_swap = seat.swap(w_mine.at[1 - half], w_in, swap_send.at[1], swap_recv.at[1])
             w_swap.start()
     total[...] = term(me)
-    for way in range(2):
-
-        @pl.when(rank(way) > 0)
-        def _():
-            hop(way, last - 1).wait_recv()
-            total[...] += came[way, last - 1].astype(F32)
+    for c in range(PARTS):
+        for way in range(2):
+
+            @pl.when(rank(way) > 0)
+            def _():
+                hop(c, way, last - 1).wait_recv()
+                total[:, c * part:(c + 1) * part] += came[c, way, last - 1].astype(F32)
 
     grad_in_ref[...] = total[...].astype(BF)
     w_swap.wait()
     grad_w_ref[...] = w_mine[half] + w_in[...]
     for tick in range(last):
-        for way in range(2):
-
-            @pl.when(sends(way, tick))
-            def _():
-                hop(way, tick).wait_send()
+        for c in range(PARTS):
+            for way in range(2):
+
+                @pl.when(sends(way, tick))
+                def _():
+                    hop(c, way, tick).wait_send()
 
     for turn in range(3):
         seat.for_mates(lambda step, to: mail(turn, step, to, place).wait_send())
@@ -462,14 +494,14 @@
             pltpu.VMEM((width, np_rows), BF),
             pltpu.VMEM((width, np_rows), BF),
             pltpu.VMEM((feats, width, np_rows), F32),
-            pltpu.VMEM((2, last, width, np_rows), BF),
-            pltpu.VMEM((2, last, width, np_rows), BF),
+            pltpu.VMEM((PARTS, 2, last, width, np_rows // PARTS), BF),
+            pltpu.VMEM((PARTS, 2, last, width, np_rows // PARTS), BF),
             pltpu.SemaphoreType.DMA((2,)),
             pltpu.SemaphoreType.DMA((2,)),
             pltpu.SemaphoreType.DMA((3, mates)),
             pltpu.SemaphoreType.DMA((3, mates)),
-            pltpu.SemaphoreType.DMA((2, last)),
-            pltpu.SemaphoreType.DMA((2, last)),
+            pltpu.SemaphoreType.DMA((PARTS, 2, last)),
+            pltpu.SemaphoreType.DMA((PARTS, 2, last)),
         ],
         compiler_params=linked(2),
     )(rows, rows_other, back, scaled_t, local_adj, grad_pre.T, w_pair, share)

time: 191 us -> 179 us (0.937)
  the two profiles are of different devices: /device:TPU:48 before, /device:TPU:6 now
where the time goes in v4:
time: 179 us; the launch traced here: 176 us
  Pallas kernels  159 us (89%)
  local copies, waits for them, and re-layouts  11.4 us (6%)
  matrix products  4.17 us (2%)
    pallas_call x1, Pallas kernels, per_device(): pl.pallas_call(forward_kernel, out_shape=(jax.ShapeDtypeStruct((feats, np...  85.3 us
    pallas_call x1, Pallas kernels, per_device(): pl.pallas_call(backward_kernel, out_shape=(jax.ShapeDtypeStruct((width, n...  72.2 us
    unnamed x37, local copies, waits for them, and re-layouts  9.53 us

profile of v4, /device:TPU:6, one launch (start us, length us, event | category | flops | bytes accessed | tf_op | source)
XLA Modules:
  0.0 176.4 jit_solution(13085749463751247640)
XLA Ops:
  0.7 2.2 %copy.37 = bf16[64,8,16,128]{3,1,2,0:T(8,128)(2,1)S(1)} copy(bf16[64,8,16,128]{3,2,1,0:T(8,128)(2,1)} %bitcast.71) | data formatting | bytes 4194304
  2.9 0.1 broadcast_in_dim.2.clone.deg_ref
  3.0 0.6 copy.38
  3.6 0.5 fusion.7.src_ref
  4.1 0.8 copy.11
  4.9 1.0 copy-done.1
  6.0 0.9 copy-done.6
  6.9 0.8 copy-done.7
  7.6 0.6 copy-done.9
  8.2 85.3 %shard_map.103 = (bf16[8,512,128]{2,1,0:T(8,128)(2,1)S(1)}, bf16[8,512,128]{2,1,0:T(8,128)(2,1)S(1)}, s32[32,128]{1,0:T(8,128)S(1)}) custom-call(s32[64]{0:T(128)S(1)} %copy-done.9, bf16[512,512]{1,0:T(8,128)(2,1)S(1)} %copy-done.1, bf16[512,128]{1,0:T(8,128)(2,1)S(1)} %copy-done.5, bf16[128,512]{1,0:T(8,128)(2,1)S(1)} %bitcast.67, ...), custom_call_target="tpu_custom_call" | custom-call | tf_op jit(solution)/shard_map/pallas_call | solution.py:431
  93.5 1.0 copy-done.3
  94.4 1.1 fusion.9
  95.5 1.2 convolution_bitcast_fusion
  96.8 0.8 copy.16
  97.5 2.0 %fusion.3 = (bf16[128,512]{1,0:T(8,128)(2,1)S(1)}, bf16[512,128]{0,1:T(8,128)(2,1)S(1)}, bf16[512,128]{0,1:T(8,128)(2,1)S(1)}) fusion(f32[512]{0:T(512)} %copy-done.13, bf16[512,128]{0,1:T(8,128)(2,1)} %copy.16, f32[512,128]{0,1:T(8,128)} %convolution_bitcast_fusion, bf16[8,512,128]{2,1,0:T(8,128)(2,1)} %copy-done.3, bf16[8,128,128]{2,1,0:T(8,128)(2,1)S(1)} %bitcast.74), kind=kOutput, calls=%fused_computation.13 | convolution fusion | flops 135266304 | bytes 2099200 | tf_op jit(solution)/shard_map/krf,kfc->rc/dot_general | solution.py:454
  99.5 0.5 fusion
  100.0 0.5 fusion.1
  100.5 0.1 pad_maximum_fusion
  100.6 0.1 copy.21
  100.7 1.3 shard_map.104.back_ref
  102.0 72.2 %shard_map.105 = (bf16[128,512]{1,0:T(8,128)(2,1)S(1)}, f32[32,128]{1,0:T(8,128)S(1)}) custom-call(s32[2,32,128]{2,1,0:T(8,128)S(1)} %bitcast.69, s32[32,128]{1,0:T(8,128)S(1)} %get-tuple-element.10.rows_other_ref, bf16[64,128,128]{2,1,0:T(8,128)(2,1)S(1)} %shard_map.104.back_ref, bf16[128,512]{1,0:T(8,128)(2,1)S(1)} %get-tuple-element.16.scaled_t_ref, ...), custom_call_target="tpu_custom_call" | custom-call | tf_op jit(solution)/shard_map/pallas_call | solution.py:479
  174.2 0.8 copy.23
  175.0 0.6 broadcast_multiply_fusion
  175.6 0.8 copy.22
  (28 shorter events, 0.1 us)
Async XLA Ops:
  0.6 2.2 %copy-start.14 = (s32[512]{0:T(512)S(1)}, s32[512]{0:T(512)}, u32[]{:S(2)}) copy-start(s32[512]{0:T(512)} %param.14) | copy-start | bytes 6148
  0.6 2.4 %copy-start.12 = (s32[1,64,128]{2,1,0:T(8,128)S(1)}, s32[1,64,128]{2,1,0:T(8,128)}, u32[]{:S(2)}) copy-start(s32[1,64,128]{2,1,0:T(8,128)} %param.10) | copy-start | bytes 98308
  0.7 3.0 %copy-start.15 = (s32[1,64]{1,0:T(1,128)S(1)}, s32[1,64]{1,0:T(1,128)}, u32[]{:S(2)}) copy-start(s32[1,64]{1,0:T(1,128)} %param.11) | copy-start | bytes 772
  0.7 3.5 %copy-start.5 = (bf16[512,128]{1,0:T(8,128)(2,1)S(1)}, bf16[512,128]{1,0:T(8,128)(2,1)}, u32[]{:S(2)}) copy-start(bf16[512,128]{1,0:T(8,128)(2,1)} %feat_ref.1) | copy-start | bytes 393220
  2.9 2.0 %copy-start.13 = (f32[512]{0:T(512)}, f32[512]{0:T(512)S(1)}, u32[]{:S(2)}) copy-start(f32[512]{0:T(512)S(1)} %convert_element_type.23) | copy-start | bytes 6148
  4.9 1.0 copy-start.1
  6.0 0.9 copy-start.6
  6.9 0.8 copy-start.7
  7.6 0.6 copy-start.9
  93.5 1.0 copy-start.3
  94.4 2.3 %copy-start.11 = (bf16[512,128]{1,0:T(8,128)(2,1)S(1)}, bf16[512,128]{1,0:T(8,128)(2,1)}, u32[]{:S(2)}) copy-start(bf16[512,128]{1,0:T(8,128)(2,1)} %param.15) | copy-start | bytes 393220
  97.5 2.0 %copy-start.4 = (bf16[8,512,128]{2,1,0:T(8,128)(2,1)S(1)}, bf16[8,512,128]{2,1,0:T(8,128)(2,1)}, u32[]{:S(2)}) copy-start(bf16[8,512,128]{2,1,0:T(8,128)(2,1)} %copy-done.3) | copy-start | bytes 3145732
  100.0 0.6 copy-start.10
  100.7 1.3 copy-start
  100.7 1.3 copy-start.2
  100.7 1.3 copy-start.8

commit v5 on v4

--- a/solution.py
+++ b/solution.py
@@ -8,7 +8,7 @@
 from jax.sharding import PartitionSpec as P
 
 BF = jnp.bfloat16
-PARTS = 2
+PARTS = 4
 F32 = jnp.float32
 VMEM_BYTES = 48 * 1024 * 1024
 PAIR = 8
@@ -17,6 +17,10 @@
 
 def vmem():
     return pl.BlockSpec(memory_space=pltpu.VMEM)
+
+
+def far():
+    return pl.BlockSpec(memory_space=pl.ANY)
 
 
 def smem():
@@ -167,9 +171,9 @@
 
 
 def forward_kernel(
-    src_ref, local_ref, feat_ref, feat_t_ref, rows_ref, tiles_ref, deg_ref,
+    src_ref, local_far, feat_ref, feat_t_ref, rows_ref, tiles_far, deg_far,
     all_feat_ref, all_agg_ref, rows_other_ref,
-    ordered, agg_ref, halo_ref, packed, other_t, rows_in, swap_send, swap_recv, mail_send, mail_recv,
+    local_ref, tiles_ref, deg_ref, near_sem, ordered, agg_ref, halo_ref, packed, other_t, rows_in, swap_send, swap_recv, mail_send, mail_recv,
     held_feat, send_feat, recv_feat, held_agg, send_agg, recv_agg,
 ):
     me = lax.axis_index("feat")
@@ -182,8 +186,16 @@
     seat.enter()
     rows_swap = seat.swap(rows_ref.at[1 - half], rows_in, swap_send.at[0], swap_recv.at[0])
     feat_swap = seat.swap(feat_t_ref, other_t, swap_send.at[1], swap_recv.at[1])
+    fetches = [
+        pltpu.make_async_copy(far, near, near_sem.at[i])
+        for i, (far, near) in enumerate(
+            [(local_far, local_ref), (tiles_far, tiles_ref), (deg_far, deg_ref)]
+        )
+    ]
     rows_swap.start()
     feat_swap.start()
+    for fetch in fetches:
+        fetch.start()
     feat_lines = gather_lines(feat_ref, held_feat, send_feat, recv_feat)
     agg_lines = gather_lines(agg_ref, held_agg, send_agg, recv_agg)
     last = feat_lines[0].last
@@ -223,6 +235,9 @@
         hand_on(feat_lines, step)
     for turn in range(2):
         seat.for_mates(lambda step, to: mail(turn, step, to, to).wait_recv())
+
+    for fetch in fetches:
+        fetch.wait()
 
     def body(b, carry):
         for t in range(span):
@@ -432,9 +447,13 @@
         forward_kernel,
         out_shape=(jax.ShapeDtypeStruct((feats, np_rows, width), BF),) * 2
         + (jax.ShapeDtypeStruct((mates, blk), jnp.int32),),
-        in_specs=[smem()] + [vmem()] * 6,
+        in_specs=[smem(), far(), vmem(), vmem(), vmem(), far(), far()],
         out_specs=(vmem(), vmem(), vmem()),
         scratch_shapes=[
+            pltpu.VMEM(local_adj.shape, BF),
+            pltpu.VMEM(tiles.shape, BF),
+            pltpu.VMEM(deg.shape, F32),
+            pltpu.SemaphoreType.DMA((3,)),
             pltpu.VMEM((width, span), BF),
             pltpu.VMEM((np_rows, width), BF),
             pltpu.VMEM((doms, width, blk), BF),

time: 179 us -> 173 us (0.966)
  Pallas kernels: 159 us -> 152 us
    pallas_call x1, Pallas kernels: 72.2 us -> 67.9 us  [per_device(): pl.pallas_call(backward_kernel, out_shape=(jax.ShapeDtypeStruct((width, n...]
    pallas_call x1, Pallas kernels: 85.3 us -> 83.3 us  [per_device(): pl.pallas_call(forward_kernel, out_shape=(jax.ShapeDtypeStruct((feats, np...]
where the time goes in v5:
time: 173 us; the launch traced here: 170 us
  Pallas kernels  152 us (88%)
  local copies, waits for them, and re-layouts  11.4 us (7%)
  matrix products  4.17 us (2%)
    pallas_call x1, Pallas kernels, per_device(): pl.pallas_call(forward_kernel, out_shape=(jax.ShapeDtypeStruct((feats, np...  83.3 us
    pallas_call x1, Pallas kernels, per_device(): pl.pallas_call(backward_kernel, out_shape=(jax.ShapeDtypeStruct((width, n...  67.9 us
    unnamed x37, local copies, waits for them, and re-layouts  9.53 us

profile of v5, /device:TPU:6, one launch (start us, length us, event | category | flops | bytes accessed | tf_op | source)
XLA Modules:
  0.0 170.0 jit_solution(588437529424239673)
XLA Ops:
  0.7 2.2 %copy.37 = bf16[64,8,16,128]{3,1,2,0:T(8,128)(2,1)S(1)} copy(bf16[64,8,16,128]{3,2,1,0:T(8,128)(2,1)} %bitcast.71) | data formatting | bytes 4194304
  2.9 0.1 broadcast_in_dim.2.clone.deg_far
  3.0 0.6 copy.38
  3.6 0.5 fusion.7.src_ref
  4.1 0.8 copy.11
  4.9 1.0 copy-done.1
  6.0 0.9 copy-done.6
  6.9 0.8 copy-done.7
  7.6 0.6 copy-done.9
  8.2 83.3 %shard_map.103 = (bf16[8,512,128]{2,1,0:T(8,128)(2,1)S(1)}, bf16[8,512,128]{2,1,0:T(8,128)(2,1)S(1)}, s32[32,128]{1,0:T(8,128)S(1)}) custom-call(s32[64]{0:T(128)S(1)} %copy-done.9, bf16[512,512]{1,0:T(8,128)(2,1)S(1)} %copy-done.1, bf16[512,128]{1,0:T(8,128)(2,1)S(1)} %copy-done.5, bf16[128,512]{1,0:T(8,128)(2,1)S(1)} %bitcast.67, ...), custom_call_target="tpu_custom_call" | custom-call | tf_op jit(solution)/shard_map/pallas_call | solution.py:446
  91.5 1.0 copy-done.3
  92.4 1.1 fusion.9
  93.5 1.2 convolution_bitcast_fusion
  94.7 0.8 copy.16
  95.5 2.0 %fusion.3 = (bf16[128,512]{1,0:T(8,128)(2,1)S(1)}, bf16[512,128]{0,1:T(8,128)(2,1)S(1)}, bf16[512,128]{0,1:T(8,128)(2,1)S(1)}) fusion(f32[512]{0:T(512)} %copy-done.13, bf16[512,128]{0,1:T(8,128)(2,1)} %copy.16, f32[512,128]{0,1:T(8,128)} %convolution_bitcast_fusion, bf16[8,512,128]{2,1,0:T(8,128)(2,1)} %copy-done.3, bf16[8,128,128]{2,1,0:T(8,128)(2,1)S(1)} %bitcast.74), kind=kOutput, calls=%fused_computation.13 | convolution fusion | flops 135266304 | bytes 2099200 | tf_op jit(solution)/shard_map/krf,kfc->rc/dot_general | solution.py:473
  97.5 0.5 fusion
  98.0 0.5 fusion.1
  98.5 0.1 pad_maximum_fusion
  98.6 0.1 copy.21
  98.7 1.3 shard_map.104.back_ref
  100.0 67.9 %shard_map.105 = (bf16[128,512]{1,0:T(8,128)(2,1)S(1)}, f32[32,128]{1,0:T(8,128)S(1)}) custom-call(s32[2,32,128]{2,1,0:T(8,128)S(1)} %bitcast.69, s32[32,128]{1,0:T(8,128)S(1)} %get-tuple-element.10.rows_other_ref, bf16[64,128,128]{2,1,0:T(8,128)(2,1)S(1)} %shard_map.104.back_ref, bf16[128,512]{1,0:T(8,128)(2,1)S(1)} %get-tuple-element.16.scaled_t_ref, ...), custom_call_target="tpu_custom_call" | custom-call | tf_op jit(solution)/shard_map/pallas_call | solution.py:498
  167.9 0.8 copy.23
  168.6 0.6 broadcast_multiply_fusion
  169.2 0.8 copy.22
  (28 shorter events, 0.1 us)
Async XLA Ops:
  0.6 2.2 %copy-start.14 = (s32[512]{0:T(512)S(1)}, s32[512]{0:T(512)}, u32[]{:S(2)}) copy-start(s32[512]{0:T(512)} %param.14) | copy-start | bytes 6148
  0.6 2.4 %copy-start.12 = (s32[1,64,128]{2,1,0:T(8,128)S(1)}, s32[1,64,128]{2,1,0:T(8,128)}, u32[]{:S(2)}) copy-start(s32[1,64,128]{2,1,0:T(8,128)} %param.10) | copy-start | bytes 98308
  0.7 3.0 %copy-start.15 = (s32[1,64]{1,0:T(1,128)S(1)}, s32[1,64]{1,0:T(1,128)}, u32[]{:S(2)}) copy-start(s32[1,64]{1,0:T(1,128)} %param.11) | copy-start | bytes 772
  0.7 3.5 %copy-start.5 = (bf16[512,128]{1,0:T(8,128)(2,1)S(1)}, bf16[512,128]{1,0:T(8,128)(2,1)}, u32[]{:S(2)}) copy-start(bf16[512,128]{1,0:T(8,128)(2,1)} %feat_ref.1) | copy-start | bytes 393220
  2.9 2.0 %copy-start.13 = (f32[512]{0:T(512)}, f32[512]{0:T(512)S(1)}, u32[]{:S(2)}) copy-start(f32[512]{0:T(512)S(1)} %convert_element_type.23) | copy-start | bytes 6148
  4.9 1.0 copy-start.1
  6.0 0.9 copy-start.6
  6.9 0.8 copy-start.7
  7.6 0.6 copy-start.9
  91.5 1.0 copy-start.3
  92.4 2.3 %copy-start.11 = (bf16[512,128]{1,0:T(8,128)(2,1)S(1)}, bf16[512,128]{1,0:T(8,128)(2,1)}, u32[]{:S(2)}) copy-start(bf16[512,128]{1,0:T(8,128)(2,1)} %param.15) | copy-start | bytes 393220
  95.5 2.0 %copy-start.4 = (bf16[8,512,128]{2,1,0:T(8,128)(2,1)S(1)}, bf16[8,512,128]{2,1,0:T(8,128)(2,1)}, u32[]{:S(2)}) copy-start(bf16[8,512,128]{2,1,0:T(8,128)(2,1)} %copy-done.3) | copy-start | bytes 3145732
  98.0 0.6 copy-start.10
  98.6 1.3 copy-start
  98.7 1.3 copy-start.2
  98.7 1.3 copy-start.8
